TPU v7x, 256 devices: a whole 4x4x8 slice. The times are simulated.
256 devices in a mesh: row: 8 (over z), col: 32 (over x, y, core).
Axes of the slice: x: 4, y: 4, z: 8, core: 2. Of those that a mesh axis runs over, the one named last changes fastest.
Arguments:
- a_trail: float32 [16384, 16384], P('row', 'col'), may hold values from -60 to 60, as said below
- a_panel: float32 [16384, 256], P(('row', 'col')), may hold values from -6 to 6
- l_panel: float32 [16384, 256], P(('row', 'col')), may hold values from -0.5 to 0.5
- a_diag: float32 [256, 256], replicated, may hold values from -60 to 60, as said below
- l_inverse: float32 [256, 256], replicated, may hold values from -4 to 4, as said below
Outputs:
- trail_out: float32 [16384, 16384], P('row', 'col')
- panel_out: float32 [16384, 256], P(('row', 'col'))
Inputs may be any that keep to these rules, and one draw needn't show every extreme that they name: `a_trail`: symmetric. `a_diag`: symmetric. `l_inverse`: lower triangular with a positive diagonal.
All inputs are finite; a program needn't handle non-finite values.
Results may differ from a plain program's by a relative error of at most 0.0003.
Values sent between devices are 32-bit elements; how exact they have to be, the bound alone decides.
No kernel may reach another device: no remote copies, remote signals or barrier semaphores. Data moves between devices by JAX's collectives and lax.ppermute only.
A program may use at most 64 MiB of HBM per device.

v0:
```python
import jax
import jax.numpy as jnp
from jax import lax
from jax.sharding import PartitionSpec as P

NS_STEPS = 8


def from_root(block, axis, owner):
    block = jnp.where(lax.axis_index(axis) == owner, block, jnp.zeros_like(block))
    return lax.psum(block, axis)


def product(left, right):
    return jnp.dot(left, right, precision=lax.Precision.HIGHEST, preferred_element_type=jnp.float32)


def newton_inverse(matrix):
    identity = jnp.eye(matrix.shape[0], dtype=jnp.float32)
    approx = identity
    for repeat in range(NS_STEPS):
        approx = product(approx, 2.0 * identity - product(matrix, approx))
    return approx


def right_solve(factor, values):
    return lax.linalg.triangular_solve(
        factor, values, left_side=False, lower=True, transpose_a=True
    )


def shards(a_trail, a_panel, l_panel, a_diag, l_inverse):
    row_dev, col_dev = a_trail.shape
    block_width = a_diag.shape[0]
    row_index = lax.axis_index("row")
    col_index = lax.axis_index("col")
    owner_row = col_index * col_dev // row_dev
    offset = col_index * col_dev - owner_row * row_dev
    a11_new = product(product(l_inverse, a_diag), l_inverse.T)
    solved = product(a_panel, l_inverse.T)
    half_term = 0.5 * product(l_panel, a11_new)
    first_y = solved - half_term
    panel_out = first_y - half_term
    y_rows, l_rows = (
        lax.all_gather(first_y, "col", axis=0, tiled=True),
        lax.all_gather(l_panel, "col", axis=0, tiled=True),
    )
    stacked = jnp.stack(
        (
            lax.dynamic_slice_in_dim(y_rows, offset, col_dev, 0),
            lax.dynamic_slice_in_dim(l_rows, offset, col_dev, 0),
        )
    )
    received = from_root(stacked, "row", owner_row)
    y_cols = received[0]
    l_cols = received[1]
    updated = a_trail - (product(y_rows, l_cols.T) + product(l_rows, y_cols.T))
    got_panel = from_root(updated[:, :block_width], "col", 0)
    global_rows = row_index * row_dev + lax.iota(jnp.int32, row_dev)
    keep_mask = (global_rows >= block_width)[:, None]
    next_panel = jnp.where(keep_mask, got_panel, 0.0)
    picker = (
        global_rows[:, None] - block_width == lax.iota(jnp.int32, block_width)[None, :]
    ).astype(jnp.float32)
    gram, top_block = lax.psum(
        (product(next_panel.T, next_panel), product(picker.T, next_panel)), "row"
    )
    factor = jnp.linalg.cholesky(gram)
    q_rows = right_solve(factor, next_panel)
    q_top = right_solve(factor, top_block)
    identity = jnp.eye(block_width, dtype=jnp.float32)
    g_inverse = newton_inverse(identity + q_top).T
    refl_rows = q_rows + picker
    refl_cols = from_root(lax.dynamic_slice_in_dim(refl_rows, offset, col_dev, 0), "row", owner_row)
    x_rows = product(lax.psum(product(updated, refl_cols), "col"), g_inverse)
    m_core = product(g_inverse.T, lax.psum(product(refl_rows.T, x_rows), "row"))
    z_rows = x_rows - 0.5 * product(refl_rows, m_core)
    z_cols = from_root(lax.dynamic_slice_in_dim(z_rows, offset, col_dev, 0), "row", owner_row)
    trail_out = updated - (product(z_rows, refl_cols.T) + product(refl_rows, z_cols.T))
    return (trail_out, panel_out)


def solution(mesh):
    return jax.shard_map(
        shards,
        mesh=mesh,
        in_specs=(P("row", "col"), P(("row", "col"), None), P(("row", "col"), None), P(), P()),
        out_specs=(P("row", "col"), P(("row", "col"), None)),
        check_vma=False,
    )
```

profile of v0, /device:TPU:1, one launch (start us, length us, event | category | flops | bytes accessed | tf_op | source)
XLA Modules:
  0.0 840.1 jit_solution(7050816020331745766)
XLA Ops:
  8.1 1.3 fusion.23
  9.9 1.1 fusion.3
  11.0 1.9 fusion.22
  13.7 52.4 %all-gather.3.cloned.1.call-done = f32[2048,256]{1,0:T(8,128)} async-done(((f32[64,256]{1,0:T(8,128)}), f32[2048,256]{1,0:T(8,128)}) %all-gather.3.cloned.1.call-update) | async-done | bytes 2097168 | tf_op jit(solution)/shard_map/all_gather | solution.py:45
  66.1 1.1 dynamic-slice_bitcast_fusion.1
  67.2 49.6 %all-gather.5.cloned.1.call-done = f32[2048,256]{1,0:T(8,128)} async-done(((f32[64,256]{1,0:T(8,128)}), f32[2048,256]{1,0:T(8,128)}) %all-gather.5.cloned.1.call-update) | async-done | bytes 2097168 | tf_op jit(solution)/shard_map/all_gather | solution.py:46
  116.8 1.1 dynamic-slice_bitcast_fusion
  117.9 1.0 maximum_select_fusion
  119.0 71.4 %all-reduce.10.cloned.1.call-done = f32[2,512,256]{2,1,0:T(8,128)} async-done(((f32[2,512,256]{2,1,0:T(8,128)}), f32[2,512,256]{2,1,0:T(8,128)}) %all-reduce.10.cloned.1.call-update) | async-done | bytes 1048592 | tf_op jit(solution)/shard_map/psum | solution.py:11
  190.4 4.7 fusion.7
  195.2 4.8 fusion
  200.0 2.0 copy-done.1
  202.0 1.6 slice_select_fusion
  204.1 119.6 %all-reduce.12.cloned.1.call-done = f32[2048,256]{1,0:T(8,128)} async-done(((f32[2048,256]{1,0:T(8,128)}), f32[2048,256]{1,0:T(8,128)}) %all-reduce.12.cloned.1.call-update) | async-done | bytes 2097168 | tf_op jit(solution)/shard_map/psum | solution.py:11
  323.7 1.9 broadcast_select_fusion
  325.7 4.2 fusion.25
  329.9 2.1 fusion.2
  332.0 65.8 %all-reduce.14.cloned.1.call-done = f32[256,256]{0,1:T(8,128)} async-done(((f32[256,256]{0,1:T(8,128)}), f32[256,256]{0,1:T(8,128)}) %all-reduce.14.cloned.1.call-update) | async-done | bytes 262160 | tf_op jit(solution)/shard_map/psum | solution.py:65
  397.8 1.1 copy.9
  398.9 1.0 fusion.8
  399.9 11.7 %cholesky.50 = f32[128,128]{1,0:T(8,128)S(1)} custom-call(f32[128,128]{1,0:T(8,128)S(1)} %cholesky.118), custom_call_target="Cholesky" | custom-call | tf_op jit(solution)/shard_map/jit(cholesky)/cholesky | solution.py:68
  411.7 9.8 %custom-call.16 = f32[1,128,128]{1,2,0:T(8,128)S(1)} custom-call(f32[1,128,128]{2,1,0:T(8,128)S(1)} %get-tuple-element.25), custom_call_target="InvertDiagBlocksLowerTriangular" | custom-call | tf_op jit(solution)/shard_map/jit(cholesky)/cholesky | solution.py:68
  422.0 11.7 %cholesky.105 = f32[128,128]{1,0:T(8,128)S(1)} custom-call(f32[128,128]{1,0:T(8,128)S(1)} %convolution_subtract_fusion.10), custom_call_target="Cholesky" | custom-call | tf_op jit(solution)/shard_map/jit(cholesky)/cholesky | solution.py:68
  435.7 4.0 while.1
  436.5 1.3 bitcast_dynamic-update-slice_fusion.2
  438.4 1.3 bitcast_dynamic-update-slice_fusion.2
  439.7 19.7 %custom-call.17 = f32[2,128,128]{1,2,0:T(8,128)S(1)} custom-call(f32[2,128,128]{2,1,0:T(8,128)S(1)} %get-tuple-element.9), custom_call_target="InvertDiagBlocksLowerTriangular" | custom-call | tf_op jit(solution)/shard_map/triangular_solve | solution.py:27
  459.4 1.1 fusion.4
  460.5 1.8 convolution_subtract_fusion
  462.3 1.1 fusion.16
  464.8 73.3 %all-reduce.22.cloned.1.call-done = (f32[512,256]{0,1:T(8,128)}, f32[256,256]{1,0:T(8,128)}) async-done(((f32[512,256]{0,1:T(8,128)}, f32[256,256]{1,0:T(8,128)}), (f32[512,256]{0,1:T(8,128)}, f32[256,256]{1,0:T(8,128)})) %all-reduce.22.cloned.1.call-update) | async-done | bytes 786448 | tf_op jit(solution)/shard_map/psum | solution.py:11
  538.2 1.2 fusion.10
  539.4 1.3 convolution_subtract_fusion.9
  544.8 1.1 convolution_subtract_fusion.3
  545.9 4.9 fusion.26
  551.1 1.3 fusion.31
  554.1 116.9 %all-reduce.16.cloned.1.call-done = f32[2048,256]{1,0:T(8,128)} async-done(((f32[2048,256]{1,0:T(8,128)}), f32[2048,256]{1,0:T(8,128)}) %all-reduce.16.cloned.1.call-update) | async-done | bytes 2097168 | tf_op jit(solution)/shard_map/psum | solution.py:75
  671.0 3.5 fusion.34
  674.5 1.3 copy-done.3
  675.8 2.6 fusion.35
  678.8 2.9 copy.13
  681.7 64.7 %all-reduce.18.cloned.1.call-done = f32[256,256]{1,0:T(8,128)} async-done(((f32[256,256]{1,0:T(8,128)}), f32[256,256]{1,0:T(8,128)}) %all-reduce.18.cloned.1.call-update) | async-done | bytes 262160 | tf_op jit(solution)/shard_map/psum | solution.py:76
  746.4 1.3 fusion.36
  747.7 3.8 fusion.1
  751.5 1.3 copy-done.4
  753.7 9.9 %fusion.37 = f32[2048,512]{1,0:T(8,128)} fusion(f32[2048,256]{0,1:T(8,128)} %copy-done.4, f32[512,256]{0,1:T(8,128)S(1)} %copy-done.8), kind=kOutput, calls=%fused_computation.84 | convolution fusion | flops 3221225472 | bytes 6815744 | tf_op jit(solution)/shard_map/dot_general | solution.py:15
  763.6 62.0 %all-reduce.20.cloned.1.call-done = f32[512,256]{0,1:T(8,128)} async-done(((f32[512,256]{0,1:T(8,128)}), f32[512,256]{0,1:T(8,128)}) %all-reduce.20.cloned.1.call-update) | async-done | bytes 524304 | tf_op jit(solution)/shard_map/psum | solution.py:11
  825.6 7.5 add_subtract_fusion
  (70 shorter events, 13.9 us)
Async XLA Ops:
  7.2 1.0 copy-start
  7.2 58.9 %all-gather.3.cloned.1.call-start = ((), (), s32[]{:S(2)}) async-start(), calls=%async_computation | async-start | bytes 2162688 | tf_op jit(solution)/shard_map/all_gather | solution.py:45
  12.9 103.9 %all-gather.5.cloned.1.call-start = ((), (), s32[]{:S(2)}) async-start(), calls=%async_computation.1 | async-start | bytes 2162688 | tf_op jit(solution)/shard_map/all_gather | solution.py:46
  13.6 176.8 %all-reduce.10.cloned.1.call-start = ((), (), s32[]{:S(2)}) async-start(), calls=%async_computation.2 | async-start | bytes 2097152 | tf_op jit(solution)/shard_map/psum | solution.py:11
  67.2 123.2 %copy-start.6 = (f32[2048,256]{1,0:T(8,128)S(1)}, f32[2048,256]{1,0:T(8,128)}, u32[]{:S(2)}) copy-start(f32[2048,256]{1,0:T(8,128)} %all-gather.3.cloned.1.call-done) | copy-start | bytes 6291460
  119.0 204.7 %all-reduce.12.cloned.1.call-start = ((), (), s32[]{:S(2)}) async-start(), calls=%async_computation.3 | async-start | bytes 4194304 | tf_op jit(solution)/shard_map/psum | solution.py:11
  190.4 4.7 copy-start.5
  190.4 4.7 copy-start.7
  200.0 2.0 copy-start.1
  203.6 194.2 %all-reduce.14.cloned.1.call-start = ((), (), s32[]{:S(2)}) async-start(), calls=%async_computation.4 | async-start | bytes 524288 | tf_op jit(solution)/shard_map/psum | solution.py:65
  329.8 208.3 %all-reduce.22.cloned.1.call-start = ((), (), s32[]{:S(2)}) async-start(), calls=%async_computation.8 | async-start | bytes 1572864 | tf_op jit(solution)/shard_map/psum | solution.py:11
  464.6 206.4 %all-reduce.16.cloned.1.call-start = ((), (), s32[]{:S(2)}) async-start(), calls=%async_computation.5 | async-start | bytes 4194304 | tf_op jit(solution)/shard_map/psum | solution.py:75
  542.8 3.1 copy-start.2
  543.2 2.7 copy-start.8
  550.8 195.6 %all-reduce.18.cloned.1.call-start = ((), (), s32[]{:S(2)}) async-start(), calls=%async_computation.6 | async-start | bytes 524288 | tf_op jit(solution)/shard_map/psum | solution.py:76
  674.5 1.3 copy-start.3
  678.5 147.2 %all-reduce.20.cloned.1.call-start = ((), (), s32[]{:S(2)}) async-start(), calls=%async_computation.7 | async-start | bytes 1048576 | tf_op jit(solution)/shard_map/psum | solution.py:11
  751.5 1.3 copy-start.4
Sparse Core Ops, SparseCore 0:
  13.0 53.0 all-gather.2
  68.7 48.1 all-gather.4
  119.8 70.6 all-reduce.9
  203.7 119.9 all-reduce.11
  330.0 67.7 all-reduce.13
  464.7 73.4 all-reduce.21
  551.0 119.9 all-reduce.15
  678.6 67.7 all-reduce.17
  753.8 71.7 all-reduce.19
where the time goes:
time: 851 us; the launch traced here: 840 us
  waiting for transfers between devices  677 us (80%)
  matrix products  68.9 us (8%)
  other arithmetic  61.2 us (7%)
  between operations  16 us (2%)
  local copies, waits for them, and re-layouts  15.7 us (2%)
    psum x4, waiting for transfers between devices, from_root(): return lax.psum(block, axis)  326 us
    psum x1, waiting for transfers between devices, shards(): x_rows = product(lax.psum(product(updated, refl_cols), 'col'), g_inverse)  117 us
    psum x1, waiting for transfers between devices, shards(): lax.psum((product(next_panel.T, next_panel), product(picker.T, next_panel...  65.8 us
    psum x1, waiting for transfers between devices, shards(): m_core = product(g_inverse.T, lax.psum(product(refl_rows.T, x_rows), 'row'))  64.7 us
    dot_general x31, matrix products, product(): jnp.dot(left, right, precision=lax.Precision.HIGHEST, preferred_element_t...  61.7 us
    all_gather x1, waiting for transfers between devices, shards(): lax.all_gather(first_y, 'col', axis=0, tiled=True)  52.4 us
    all_gather x1, waiting for transfers between devices, shards(): lax.all_gather(l_panel, 'col', axis=0, tiled=True)  49.6 us
    another operation x6, other arithmetic, shards(): factor = jnp.linalg.cholesky(gram)  34 us
  transfers between devices with their start and end apart: 9, of which 9 were waited for; matrix products, arithmetic and copies ran while one was open for 2% of the time, Pallas kernels for 0%

commit v1 on v0

v1 whole, which is shorter than its diff:
```python
import functools

import jax
import jax.numpy as jnp
from jax import lax
from jax.experimental import pallas as pl
from jax.experimental.pallas import tpu as pltpu
from jax.sharding import PartitionSpec as P

NS_STEPS = 8
ROWS = 8
COLS = 32
BOTH = ("row", "col")


def product(left, right):
    return jnp.dot(left, right, precision=lax.Precision.HIGHEST, preferred_element_type=jnp.float32)


def product3(left, right):
    return jnp.dot(left, right, precision=lax.Precision.HIGH, preferred_element_type=jnp.float32)


def right_solve(factor, values):
    return lax.linalg.triangular_solve(
        factor, values, left_side=False, lower=True, transpose_a=True
    )


def newton_inverse_of_shifted(top):
    size = top.shape[0]
    residual = -top
    approx = jnp.eye(size, dtype=jnp.float32) + residual
    for step in range(1, NS_STEPS):
        residual = product(residual, residual)
        approx = approx + product(approx, residual)
    return approx


def place(pieces, offsets, out_rows):
    arrays = []
    where = []
    for array, start, size in pieces:
        for at, known in enumerate(arrays):
            if known is array:
                break
        else:
            at = len(arrays)
            arrays.append(array)
        where.append((at, start, size))
    width = arrays[0].shape[1]
    count = len(where)

    def body(offs, *refs):
        sources = refs[: len(arrays)]
        out = refs[len(arrays)]
        sems = refs[len(arrays) + 1]
        copies = []
        for index, (at, start, size) in enumerate(where):
            copy = pltpu.make_async_copy(
                sources[at].at[pl.ds(start, size)],
                out.at[pl.ds(pl.multiple_of(offs[index], 8), size)],
                sems.at[index],
            )
            copy.start()
            copies.append(copy)
        for copy in copies:
            copy.wait()

    return pl.pallas_call(
        body,
        out_shape=jax.ShapeDtypeStruct((out_rows, width), jnp.float32),
        in_specs=[pl.BlockSpec(memory_space=pltpu.SMEM)] + [pl.BlockSpec(memory_space=pl.ANY)] * len(arrays),
        out_specs=pl.BlockSpec(memory_space=pl.ANY),
        scratch_shapes=[pltpu.SemaphoreType.DMA((count,))],
    )(jnp.stack(offsets).astype(jnp.int32), *arrays)


def col_shift(first_axis, step):
    def target(col):
        x, y, core = col // 8, (col // 2) % 4, col % 2
        if (core == 0) == first_axis:
            x = (x + step) % 4
        else:
            y = (y + step) % 4
        return x * 8 + y * 2 + core

    return [(col, target(col)) for col in range(COLS)]


def gather_cols(block):
    rows = block.shape[0]
    move = functools.partial(lax.ppermute, axis_name="col")

    def ring(value, first_axis):
        return [
            value,
            move(value, perm=col_shift(first_axis, -1)),
            move(value, perm=col_shift(first_axis, 2)),
            move(value, perm=col_shift(first_axis, 1)),
        ]

    own = ring(jnp.concatenate(ring(block, True), 0), False)
    other = [move(value, perm=[(col, col ^ 1) for col in range(COLS)]) for value in own]
    col = lax.axis_index("col")
    x, y, core = col // 8, (col // 2) % 4, col % 2
    pieces, offsets = [], []
    for values, its_core in ((own, core), (other, 1 - core)):
        for second in range(4):
            for first in range(4):
                step_x = jnp.where(its_core == 0, first, second)
                step_y = jnp.where(its_core == 0, second, first)
                at = ((x + step_x) % 4) * 8 + ((y + step_y) % 4) * 2 + its_core
                pieces.append((values[second], first * rows, rows))
                offsets.append(at * rows)
    return place(pieces, offsets, COLS * rows)


def gather_rows(block):
    rows = block.shape[0]
    row = lax.axis_index("row")
    pieces, offsets = [(block, 0, rows)], [row * rows]
    for step in range(1, ROWS):
        got = lax.ppermute(block, "row", [(at, (at + step) % ROWS) for at in range(ROWS)])
        pieces.append((got, 0, rows))
        offsets.append(((row - step) % ROWS) * rows)
    return place(pieces, offsets, ROWS * rows)


def to_columns(block):
    return lax.ppermute(
        block, BOTH, [(at, (at % 8) * COLS + at // 8) for at in range(ROWS * COLS)]
    )


def sum_rows(block):
    total = block
    for step in range(1, ROWS):
        total = total + lax.ppermute(block, "row", [(at, (at + step) % ROWS) for at in range(ROWS)])
    return total


def from_first_row(block):
    row = lax.axis_index("row")
    total = jnp.where(row == 0, block, 0.0)
    for step in range(1, ROWS):
        total = total + lax.ppermute(block, "row", [(0, step)])
    return total


def scatter_sum_cols(block):
    parts = lax.all_to_all(block, "col", 0, 0, tiled=True)
    return jnp.sum(parts.reshape(COLS, block.shape[0] // COLS, block.shape[1]), axis=0)


def shards(a_trail, a_panel, l_panel, a_diag, l_inverse):
    row_dev, col_dev = a_trail.shape
    nb = a_diag.shape[0]
    part = col_dev // ROWS
    row = lax.axis_index("row")
    col = lax.axis_index("col")

    raw_rows = gather_cols(jnp.concatenate([a_panel, l_panel], 1))

    a11_new = product(product(l_inverse, a_diag), l_inverse.T)
    half_term = 0.5 * product(l_panel, a11_new)
    first_y = product(a_panel, l_inverse.T) - half_term
    panel_out = first_y - half_term
    mates = gather_rows(to_columns(jnp.concatenate([product(l_panel, l_inverse), panel_out], 1)))
    updated = a_trail - product3(raw_rows, mates.T)

    local = lax.iota(jnp.int32, col_dev)
    not_top = jnp.logical_or(col > 0, local >= nb)
    head = updated[: 2 * nb]
    panel_t = jnp.where(not_top[None, :], head[:nb], 0.0)

    corner = jnp.where(col == 0, head[nb:], 0.0)
    packed = from_first_row(
        scatter_sum_cols(jnp.concatenate([product(panel_t, panel_t.T), corner], 1))
    )
    packed = gather_cols(packed)
    gram, top_block, corner = packed[:, :nb], packed[:, nb : 2 * nb], packed[:, 2 * nb :]

    flipped = jnp.concatenate([panel_t, head[nb:]], 0).T
    shard = None
    for at in range(ROWS):
        got = lax.ppermute(
            flipped[at * part : (at + 1) * part],
            BOTH,
            [(c, (c // 4) * COLS + (c % 4) * 8 + at) for c in range(COLS)],
        )
        shard = got if shard is None else shard + got
    both_rows = gather_cols(shard)
    both_cols = gather_rows(to_columns(shard))
    panel_rows, second_rows = both_rows[:, :nb], both_rows[:, nb:]
    panel_cols, second_cols = both_cols[:, :nb], both_cols[:, nb:]

    partial = product3(updated.T, panel_rows)
    image = None
    for step in range(ROWS):
        at = (row + step) % ROWS
        got = lax.ppermute(
            lax.dynamic_slice_in_dim(partial, at * part, part, 0),
            BOTH,
            [
                (r * COLS + c, (c // 4) * COLS + (c % 4) * 8 + (r + step) % ROWS)
                for r in range(ROWS)
                for c in range(COLS)
            ],
        )
        image = got if image is None else image + got
    image_rows = gather_cols(image)
    image_cols = gather_rows(to_columns(image))

    weights = jnp.concatenate(
        [product3(panel_cols.T, partial), jnp.where(col == 0, partial[nb : 2 * nb], 0.0)], 1
    )
    weights = gather_cols(sum_rows(scatter_sum_cols(weights)))
    core, image_top = weights[:, :nb], weights[:, nb:]

    factor = jnp.linalg.cholesky(gram)
    solve = right_solve(factor, jnp.eye(nb, dtype=jnp.float32))
    g_inverse = newton_inverse_of_shifted(product(top_block, solve)).T
    image_top = product(image_top, solve)
    middle = product(product(solve.T, core), solve) + image_top + image_top.T + corner
    m_core = product(g_inverse.T, product(middle, g_inverse))
    solve_g = product(solve, g_inverse)

    def reflectors(panel, image, second, owner):
        size = panel.shape[0]
        picker = jnp.logical_and(
            lax.iota(jnp.int32, size)[:, None] - nb == lax.iota(jnp.int32, nb)[None, :], owner
        ).astype(jnp.float32)
        y_part = product3(panel, solve) + picker
        x_part = product3(image, solve_g) + product3(second, g_inverse)
        return y_part, x_part - 0.5 * product3(y_part, m_core)

    y_rows, z_rows = reflectors(panel_rows, image_rows, second_rows, row == 0)
    y_cols, z_cols = reflectors(panel_cols, image_cols, second_cols, col == 0)
    trail_out = updated - product3(
        jnp.concatenate([z_rows, y_rows], 1), jnp.concatenate([y_cols, z_cols], 1).T
    )
    return (trail_out, panel_out)


def solution(mesh):
    return jax.shard_map(
        shards,
        mesh=mesh,
        in_specs=(P("row", "col"), P(("row", "col"), None), P(("row", "col"), None), P(), P()),
        out_specs=(P("row", "col"), P(("row", "col"), None)),
        check_vma=False,
    )
```

time: 851 us -> 1000 us (1.18)
  waiting for transfers between devices: 677 us -> 47.4 us
  Pallas kernels: 0 us -> 453 us
  starting transfers between devices: 1.59 us -> 358 us
  matrix products: 68.9 us -> 46.2 us
  local copies, waits for them, and re-layouts: 15.7 us -> 28.7 us
  between operations: 16 us -> 4.62 us
    psum x7 -> x0, waiting for transfers between devices: 574 us -> none  [the longest x4 326 us: from_root(): return lax.psum(block, axis)]
    pallas_call x0 -> x8, Pallas kernels: none -> 453 us  [place(): pl.pallas_call(body, out_shape=jax.ShapeDtypeStruct((out_rows, width), jn...]
    ppermute x0 -> x104, starting transfers between devices: none -> 346 us  [the longest x8 94.4 us: shards(): lax.ppermute(lax.dynamic_slice_in_dim(partial, at * part, part, 0), BOTH,...]
    all_gather x2 -> x0, waiting for transfers between devices: 102 us -> none  [the longest x1 52.4 us: shards(): lax.all_gather(first_y, 'col', axis=0, tiled=True)]
    ppermute x0 -> x104, waiting for transfers between devices: none -> 47.4 us  [the longest x21 22.8 us: gather_rows(): lax.ppermute(block, 'row', [(at, (at + step) % ROWS) for at in range(ROWS)])]
    dot_general x31 -> x27, matrix products: 61.7 us -> 19.2 us  [product(): jnp.dot(left, right, precision=lax.Precision.HIGHEST, preferred_element_t...]
    dot_general x0 -> x12, matrix products: none -> 25.6 us  [product3(): jnp.dot(left, right, precision=lax.Precision.HIGH, preferred_element_type...]
    all_to_all x0 -> x2, starting transfers between devices: none -> 11.8 us  [scatter_sum_cols(): parts = lax.all_to_all(block, 'col', 0, 0, tiled=True)]
  transfers between devices with their start and end apart: 9 -> 106, of which waited for: 9 -> 15; matrix products, arithmetic and copies ran while one was open for 2% -> 9% of each run, Pallas kernels for 0% -> 18%
where the time goes in v1:
time: 1000 us; the launch traced here: 995 us
  Pallas kernels  453 us (45%)
  starting transfers between devices  358 us (36%)
  other arithmetic  57.2 us (6%)
  waiting for transfers between devices  47.4 us (5%)
  matrix products  46.2 us (5%)
  local copies, waits for them, and re-layouts  28.7 us (3%)
    pallas_call x8, Pallas kernels, place(): pl.pallas_call(body, out_shape=jax.ShapeDtypeStruct((out_rows, width), jn...  453 us
    ppermute x8, starting transfers between devices, shards(): lax.ppermute(lax.dynamic_slice_in_dim(partial, at * part, part, 0), BOTH,...  94.4 us
    ppermute x21, starting transfers between devices, gather_rows(): lax.ppermute(block, 'row', [(at, (at + step) % ROWS) for at in range(ROWS)])  61.8 us
    ppermute x20, starting transfers between devices, gather_cols(): move(value, perm=[(col, col ^ 1) for col in range(COLS)])  34.7 us
    another operation x6, other arithmetic, shards(): factor = jnp.linalg.cholesky(gram)  34 us
    ppermute x10, starting transfers between devices, ring(): move(value, perm=col_shift(first_axis, 2))  33.8 us
    dot_general x12, matrix products, product3(): jnp.dot(left, right, precision=lax.Precision.HIGH, preferred_element_type...  25.6 us
    ppermute x10, starting transfers between devices, ring(): move(value, perm=col_shift(first_axis, -1))  25.5 us
  transfers between devices with their start and end apart: 106, of which 15 were waited for; matrix products, arithmetic and copies ran while one was open for 9% of the time, Pallas kernels for 18%

profile of v1, /device:TPU:1, one launch (start us, length us, event | category | flops | bytes accessed | tf_op | source)
XLA Modules:
  0.0 994.8 jit_solution(8732063968975268435)
XLA Ops:
  16.8 6.0 collective-permute-start.10
  22.8 5.2 collective-permute-done.10.refs_0_
  27.9 10.8 %collective-permute-start.17 = (f32[64,512]{1,0:T(8,128)S(1)}, f32[64,512]{1,0:T(8,128)S(1)}, u32[]{:S(2)}, u32[]{:S(2)}) collective-permute-start(f32[64,512]{1,0:T(8,128)S(1)} %collective-permute-done.10.refs_0_), channel_id=1, source_target_pairs={{0,224},{32,0},{64,32},{96,64},{128,96},{160,128},{192,160},{224,1... | collective-permute-start | bytes 393224 | tf_op jit(solution)/shard_map/ppermute | solution.py:124
  49.7 8.6 collective-permute-start.6
  58.9 9.1 collective-permute-start.13
  68.1 7.5 collective-permute-done.13.refs_3_
  76.8 5.8 collective-permute-done.12.refs_2_
  87.0 5.3 copy.15
  94.4 33.6 %shard_map.69 = f32[512,512]{1,0:T(8,128)} custom-call(s32[8]{0:T(128)} %stack.191.offs, f32[64,512]{1,0:T(8,128)} %copy-done.29, f32[64,512]{1,0:T(8,128)} %copy-done.36, f32[64,512]{1,0:T(8,128)} %copy-done.35, f32[64,512]{1,0:T(8,128)} %copy-done.34, f32[64,512]{1,0:T(8,128)} %copy-done.33, f32[64,512]{1,0:T(8,128)} %copy-done.32, f32[64,512]{1,0:T(8,128)} %copy-done.31, ...), custom_call_target="tpu_custom_call" | custom-call | tf_op jit(solution)/shard_map/pallas_call | solution.py:70
  128.0 129.2 %shard_map.68 = f32[2048,512]{1,0:T(8,128)} custom-call(s32[32]{0:T(128)} %stack.182.offs, f32[256,512]{1,0:T(8,128)} %copy-done.9, f32[256,512]{1,0:T(8,128)} %copy-done.17, f32[256,512]{1,0:T(8,128)} %copy-done.16, f32[256,512]{1,0:T(8,128)} %copy-done.15, f32[256,512]{1,0:T(8,128)} %collective-permute-done.6.refs_4_, ...), custom_call_target="tpu_custom_call" | custom-call | tf_op jit(solution)/shard_map/pallas_call | solution.py:70
  257.3 6.5 convolution_subtract_fusion
  267.1 6.4 all-to-all-start
  276.9 7.9 collective-permute-start.25
  295.2 11.0 %collective-permute-start.71 = (f32[64,512]{1,0:T(8,128)S(1)}, f32[64,512]{1,0:T(8,128)S(1)}, u32[]{:S(2)}, u32[]{:S(2)}) collective-permute-start(f32[64,512]{1,0:T(8,128)S(1)} %add_add_fusion), channel_id=1, source_target_pairs={{0,0},{1,32},{2,64},{3,96},{4,128},{5,160},{6,192},{7,224},{8,1},{... | collective-permute-start | bytes 393224 | tf_op jit(solution)/shard_map/ppermute | solution.py:131
  306.2 5.9 collective-permute-start.28
  312.1 5.4 collective-permute-start.27
  319.6 5.2 collective-permute-start.60
  342.4 5.6 collective-permute-start.29
  351.3 4.6 collective-permute-start.62
  363.3 14.3 %collective-permute-start.66 = (f32[32,768]{1,0:T(8,128)S(1)}, f32[32,768]{1,0:T(8,128)S(1)}, u32[]{:S(2)}, u32[]{:S(2)}) collective-permute-start(f32[32,768]{1,0:T(8,128)S(1)} %pad_maximum_fusion.6.refs_0_), channel_id=1, source_target_pairs={{0,2},{1,9},{2,4},{3,11},{4,6},{5,13},{6,0},{7,15},{8,10},{9,17},{... | collective-permute-start | bytes 294920 | tf_op jit(solution)/shard_map/ppermute | solution.py:100
  377.6 11.8 %collective-permute-start.65 = (f32[32,768]{1,0:T(8,128)S(1)}, f32[32,768]{1,0:T(8,128)S(1)}, u32[]{:S(2)}, u32[]{:S(2)}) collective-permute-start(f32[32,768]{1,0:T(8,128)S(1)} %pad_maximum_fusion.6.refs_0_), channel_id=1, source_target_pairs={{0,4},{1,17},{2,6},{3,19},{4,0},{5,21},{6,2},{7,23},{8,12},{9,25},... | collective-permute-start | bytes 294920 | tf_op jit(solution)/shard_map/ppermute | solution.py:99
  389.4 11.8 %collective-permute-start.64 = (f32[32,768]{1,0:T(8,128)S(1)}, f32[32,768]{1,0:T(8,128)S(1)}, u32[]{:S(2)}, u32[]{:S(2)}) collective-permute-start(f32[32,768]{1,0:T(8,128)S(1)} %pad_maximum_fusion.6.refs_0_), channel_id=1, source_target_pairs={{0,6},{1,25},{2,0},{3,27},{4,2},{5,29},{6,4},{7,31},{8,14},{9,1},{... | collective-permute-start | bytes 294920 | tf_op jit(solution)/shard_map/ppermute | solution.py:98
  403.5 10.2 %collective-permute-start.69 = (f32[32,768]{1,0:T(8,128)S(1)}, f32[32,768]{1,0:T(8,128)}, u32[]{:S(2)}, u32[]{:S(2)}) collective-permute-start(f32[32,768]{1,0:T(8,128)S(1)} %collective-permute-done.65.refs_2_), channel_id=1, source_target_pairs={{0,1},{1,0},{2,3},{3,2},{4,5},{5,4},{6,7},{7,6},{8,9},{9,8},{10,11... | collective-permute-start | bytes 294920 | tf_op jit(solution)/shard_map/ppermute | solution.py:104
  415.9 33.6 %shard_map.73 = f32[512,512]{1,0:T(8,128)} custom-call(s32[8]{0:T(128)} %stack.191.offs, f32[64,512]{1,0:T(8,128)} %copy-done.37, f32[64,512]{1,0:T(8,128)} %copy-done.44, f32[64,512]{1,0:T(8,128)} %copy-done.43, f32[64,512]{1,0:T(8,128)} %copy-done.42, f32[64,512]{1,0:T(8,128)} %copy-done.41, f32[64,512]{1,0:T(8,128)} %copy-done.40, f32[64,512]{1,0:T(8,128)} %copy-done.39, ...), custom_call_target="tpu_custom_call" | custom-call | tf_op jit(solution)/shard_map/pallas_call | solution.py:70
  450.9 25.9 %shard_map.72 = f32[256,768]{1,0:T(8,128)} custom-call(s32[32]{0:T(128)} %stack.416.offs, f32[32,768]{1,0:T(8,128)} %copy-done.20, f32[32,768]{1,0:T(8,128)} %copy-done.47, f32[32,768]{1,0:T(8,128)} %copy-done.46, f32[32,768]{1,0:T(8,128)} %copy-done.45, f32[32,768]{1,0:T(8,128)} %copy-done.48, f32[32,768]{1,0:T(8,128)} %collective-permute-done.68.refs_5_, ...), custom_call_target="tpu_custom_call" | custom-call | tf_op jit(solution)/shard_map/pallas_call | solution.py:70
  478.9 11.7 %cholesky.50 = f32[128,128]{1,0:T(8,128)S(1)} custom-call(f32[128,128]{1,0:T(8,128)S(1)} %cholesky.118), custom_call_target="Cholesky" | custom-call | tf_op jit(solution)/shard_map/jit(cholesky)/cholesky | solution.py:221
  490.7 9.8 custom-call.14
  501.0 11.7 %cholesky.105 = f32[128,128]{1,0:T(8,128)S(1)} custom-call(f32[128,128]{1,0:T(8,128)S(1)} %slice_subtract_fusion), custom_call_target="Cholesky" | custom-call | tf_op jit(solution)/shard_map/jit(cholesky)/cholesky | solution.py:221
  514.9 5.8 while.1
  520.6 20.5 %custom-call.15 = f32[2,128,128]{1,2,0:T(8,128)S(1)} custom-call(f32[2,128,128]{2,1,0:T(8,128)} %get-tuple-element.9), custom_call_target="InvertDiagBlocksLowerTriangular" | custom-call | tf_op jit(solution)/shard_map/triangular_solve | solution.py:25
  548.2 129.1 %shard_map.70 = f32[2048,512]{1,0:T(8,128)} custom-call(s32[32]{0:T(128)} %stack.182.offs, f32[256,512]{1,0:T(8,128)} %copy-done.10, f32[256,512]{1,0:T(8,128)} %collective-permute-done.29.refs_1_, f32[256,512]{1,0:T(8,128)} %copy-done.19, f32[256,512]{1,0:T(8,128)} %copy-done.18, f32[256,512]{1,0:T(8,128)} %collective-permute-done.32.refs_4_, ...), custom_call_target="tpu_custom_call" | custom-call | tf_op jit(solution)/shard_map/pallas_call | solution.py:70
  677.3 4.8 fusion.12
  683.6 5.4 all-to-all-start.1
  689.1 13.1 %collective-permute-start.37 = (f32[64,256]{1,0:T(8,128)S(1)}, f32[64,256]{1,0:T(8,128)S(1)}, u32[]{:S(2)}, u32[]{:S(2)}) collective-permute-start(f32[64,256]{1,0:T(8,128)S(1)} %get-tuple-element.35), channel_id=1, source_target_pairs={{0,1},{1,9},{2,17},{3,25},{4,33},{5,41},{6,49},{7,57},{8,65},{9,73... | collective-permute-start | bytes 196616 | tf_op jit(solution)/shard_map/ppermute | solution.py:202
  702.2 13.1 %collective-permute-start.43 = (f32[64,256]{1,0:T(8,128)S(1)}, f32[64,256]{1,0:T(8,128)S(1)}, u32[]{:S(2)}, u32[]{:S(2)}) collective-permute-start(f32[64,256]{1,0:T(8,128)S(1)} %get-tuple-element.36), channel_id=1, source_target_pairs={{0,7},{1,15},{2,23},{3,31},{4,39},{5,47},{6,55},{7,63},{8,71},{9,7... | collective-permute-start | bytes 196616 | tf_op jit(solution)/shard_map/ppermute | solution.py:202
  715.4 13.1 %collective-permute-start.42 = (f32[64,256]{1,0:T(8,128)S(1)}, f32[64,256]{1,0:T(8,128)S(1)}, u32[]{:S(2)}, u32[]{:S(2)}) collective-permute-start(f32[64,256]{1,0:T(8,128)S(1)} %get-tuple-element.37), channel_id=1, source_target_pairs={{0,6},{1,14},{2,22},{3,30},{4,38},{5,46},{6,54},{7,62},{8,70},{9,7... | collective-permute-start | bytes 196616 | tf_op jit(solution)/shard_map/ppermute | solution.py:202
  728.9 13.1 %collective-permute-start.41 = (f32[64,256]{1,0:T(8,128)S(1)}, f32[64,256]{1,0:T(8,128)S(1)}, u32[]{:S(2)}, u32[]{:S(2)}) collective-permute-start(f32[64,256]{1,0:T(8,128)S(1)} %get-tuple-element.38), channel_id=1, source_target_pairs={{0,5},{1,13},{2,21},{3,29},{4,37},{5,45},{6,53},{7,61},{8,69},{9,7... | collective-permute-start | bytes 196616 | tf_op jit(solution)/shard_map/ppermute | solution.py:202
  742.0 11.9 %collective-permute-start.40 = (f32[64,256]{1,0:T(8,128)S(1)}, f32[64,256]{1,0:T(8,128)S(1)}, u32[]{:S(2)}, u32[]{:S(2)}) collective-permute-start(f32[64,256]{1,0:T(8,128)S(1)} %get-tuple-element.39), channel_id=1, source_target_pairs={{0,4},{1,12},{2,20},{3,28},{4,36},{5,44},{6,52},{7,60},{8,68},{9,7... | collective-permute-start | bytes 196616 | tf_op jit(solution)/shard_map/ppermute | solution.py:202
  753.9 13.1 %collective-permute-start.39 = (f32[64,256]{1,0:T(8,128)S(1)}, f32[64,256]{1,0:T(8,128)S(1)}, u32[]{:S(2)}, u32[]{:S(2)}) collective-permute-start(f32[64,256]{1,0:T(8,128)S(1)} %get-tuple-element.40), channel_id=1, source_target_pairs={{0,3},{1,11},{2,19},{3,27},{4,35},{5,43},{6,51},{7,59},{8,67},{9,7... | collective-permute-start | bytes 196616 | tf_op jit(solution)/shard_map/ppermute | solution.py:202
  767.1 13.3 %collective-permute-start.38 = (f32[64,256]{1,0:T(8,128)S(1)}, f32[64,256]{1,0:T(8,128)S(1)}, u32[]{:S(2)}, u32[]{:S(2)}) collective-permute-start(f32[64,256]{1,0:T(8,128)S(1)} %get-tuple-element.41), channel_id=1, source_target_pairs={{0,2},{1,10},{2,18},{3,26},{4,34},{5,42},{6,50},{7,58},{8,66},{9,7... | collective-permute-start | bytes 196616 | tf_op jit(solution)/shard_map/ppermute | solution.py:202
  784.4 11.4 %collective-permute-done.38 = f32[64,256]{1,0:T(8,128)S(1)} collective-permute-done((f32[64,256]{1,0:T(8,128)S(1)}, f32[64,256]{1,0:T(8,128)S(1)}, u32[]{:S(2)}, u32[]{:S(2)}) %collective-permute-start.38) | collective-permute-done | bytes 65568 | tf_op jit(solution)/shard_map/ppermute | solution.py:202
  799.8 9.8 collective-permute-start.85
  810.9 5.5 collective-permute-start.82
  867.0 17.7 %shard_map.75 = f32[512,256]{1,0:T(8,128)} custom-call(s32[8]{0:T(128)} %stack.191.offs, f32[64,256]{1,0:T(8,128)} %copy-done.49, f32[64,256]{1,0:T(8,128)} %copy-done.56, f32[64,256]{1,0:T(8,128)} %copy-done.55, f32[64,256]{1,0:T(8,128)} %copy-done.54, f32[64,256]{1,0:T(8,128)} %copy-done.53, f32[64,256]{1,0:T(8,128)} %copy-done.52, f32[64,256]{1,0:T(8,128)} %copy-done.51, ...), custom_call_target="tpu_custom_call" | custom-call | tf_op jit(solution)/shard_map/pallas_call | solution.py:70
  884.8 65.6 %shard_map.71 = f32[2048,256]{1,0:T(8,128)} custom-call(s32[32]{0:T(128)} %stack.182.offs, f32[256,256]{1,0:T(8,128)} %copy-done.13, f32[256,256]{1,0:T(8,128)} %collective-permute-done.47.refs_1_, f32[256,256]{1,0:T(8,128)} %copy-done.23, f32[256,256]{1,0:T(8,128)} %copy-done.22, f32[256,256]{1,0:T(8,128)} %copy-done.21, ...), custom_call_target="tpu_custom_call" | custom-call | tf_op jit(solution)/shard_map/pallas_call | solution.py:70
  951.0 17.9 %shard_map.74 = f32[256,512]{1,0:T(8,128)} custom-call(s32[32]{0:T(128)} %stack.416.offs, f32[32,512]{1,0:T(8,128)} %copy-done.28, f32[32,512]{1,0:T(8,128)} %collective-permute-done.89.refs_1_, f32[32,512]{1,0:T(8,128)} %collective-permute-done.90.refs_2_, f32[32,512]{1,0:T(8,128)} %collective-permute-done.91.refs_3_, f32[32,512]{1,0:T(8,128)} %copy-done.57, ...), custom_call_target="tpu_custom_call" | custom-call | tf_op jit(solution)/shard_map/pallas_call | solution.py:70
  983.8 5.2 fusion.4
  989.0 5.4 copy.23
  (388 shorter events, 180.1 us)
Async XLA Ops:
  11.6 46.7 %collective-permute-start.5 = (f32[256,512]{1,0:T(8,128)S(1)}, f32[256,512]{1,0:T(8,128)S(1)}, u32[]{:S(2)}, u32[]{:S(2)}) collective-permute-start(f32[256,512]{1,0:T(8,128)S(1)} %pad_maximum_fusion.1.refs_0_), channel_id=1, source_target_pairs={{0,2},{1,9},{2,4},{3,11},{4,6},{5,13},{6,0},{7,15},{8,10},{9,17},{... | collective-permute-start | bytes 1572872 | tf_op jit(solution)/shard_map/ppermute | solution.py:100
  12.9 45.5 %collective-permute-start.4 = (f32[256,512]{1,0:T(8,128)S(1)}, f32[256,512]{1,0:T(8,128)S(1)}, u32[]{:S(2)}, u32[]{:S(2)}) collective-permute-start(f32[256,512]{1,0:T(8,128)S(1)} %pad_maximum_fusion.1.refs_0_), channel_id=1, source_target_pairs={{0,4},{1,17},{2,6},{3,19},{4,0},{5,21},{6,2},{7,23},{8,12},{9,25},... | collective-permute-start | bytes 1572872 | tf_op jit(solution)/shard_map/ppermute | solution.py:99
  15.3 43.5 %collective-permute-start.3 = (f32[256,512]{1,0:T(8,128)S(1)}, f32[256,512]{1,0:T(8,128)S(1)}, u32[]{:S(2)}, u32[]{:S(2)}) collective-permute-start(f32[256,512]{1,0:T(8,128)S(1)} %pad_maximum_fusion.1.refs_0_), channel_id=1, source_target_pairs={{0,6},{1,25},{2,0},{3,27},{4,2},{5,29},{6,4},{7,31},{8,14},{9,1},{... | collective-permute-start | bytes 1572872 | tf_op jit(solution)/shard_map/ppermute | solution.py:98
  44.8 14.1 %collective-permute-start.14 = (f32[64,512]{1,0:T(8,128)S(1)}, f32[64,512]{1,0:T(8,128)S(1)}, u32[]{:S(2)}, u32[]{:S(2)}) collective-permute-start(f32[64,512]{1,0:T(8,128)S(1)} %collective-permute-done.10.refs_0_), channel_id=1, source_target_pairs={{0,128},{32,160},{64,192},{96,224},{128,0},{160,32},{192,64},{224,... | collective-permute-start | bytes 393224 | tf_op jit(solution)/shard_map/ppermute | solution.py:124
  49.7 78.3 %collective-permute-start.6 = (f32[256,512]{1,0:T(8,128)S(1)}, f32[256,512]{1,0:T(8,128)}, u32[]{:S(2)}, u32[]{:S(2)}) collective-permute-start(f32[256,512]{1,0:T(8,128)S(1)} %pad_maximum_fusion.1.refs_0_), channel_id=1, source_target_pairs={{0,1},{1,0},{2,3},{3,2},{4,5},{5,4},{6,7},{7,6},{8,9},{9,8},{10,11... | collective-permute-start | bytes 1572872 | tf_op jit(solution)/shard_map/ppermute | solution.py:104
  58.3 69.7 %collective-permute-start.9 = (f32[256,512]{1,0:T(8,128)S(1)}, f32[256,512]{1,0:T(8,128)}, u32[]{:S(2)}, u32[]{:S(2)}) collective-permute-start(f32[256,512]{1,0:T(8,128)S(1)} %collective-permute-done.5.refs_3_), channel_id=1, source_target_pairs={{0,1},{1,0},{2,3},{3,2},{4,5},{5,4},{6,7},{7,6},{8,9},{9,8},{10,11... | collective-permute-start | bytes 1572872 | tf_op jit(solution)/shard_map/ppermute | solution.py:104
  58.4 69.6 %collective-permute-start.8 = (f32[256,512]{1,0:T(8,128)S(1)}, f32[256,512]{1,0:T(8,128)}, u32[]{:S(2)}, u32[]{:S(2)}) collective-permute-start(f32[256,512]{1,0:T(8,128)S(1)} %collective-permute-done.4.refs_2_), channel_id=1, source_target_pairs={{0,1},{1,0},{2,3},{3,2},{4,5},{5,4},{6,7},{7,6},{8,9},{9,8},{10,11... | collective-permute-start | bytes 1572872 | tf_op jit(solution)/shard_map/ppermute | solution.py:104
  58.8 69.2 %collective-permute-start.7 = (f32[256,512]{1,0:T(8,128)S(1)}, f32[256,512]{1,0:T(8,128)}, u32[]{:S(2)}, u32[]{:S(2)}) collective-permute-start(f32[256,512]{1,0:T(8,128)S(1)} %collective-permute-done.3.refs_1_), channel_id=1, source_target_pairs={{0,1},{1,0},{2,3},{3,2},{4,5},{5,4},{6,7},{7,6},{8,9},{9,8},{10,11... | collective-permute-start | bytes 1572872 | tf_op jit(solution)/shard_map/ppermute | solution.py:104
  58.9 16.6 %collective-permute-start.13 = (f32[64,512]{1,0:T(8,128)S(1)}, f32[64,512]{1,0:T(8,128)S(1)}, u32[]{:S(2)}, u32[]{:S(2)}) collective-permute-start(f32[64,512]{1,0:T(8,128)S(1)} %collective-permute-done.10.refs_0_), channel_id=1, source_target_pairs={{0,96},{32,128},{64,160},{96,192},{128,224},{160,0},{192,32},{224,... | collective-permute-start | bytes 393224 | tf_op jit(solution)/shard_map/ppermute | solution.py:124
  267.1 52.4 %all-to-all-start = ((f32[32,8,768]{2,1,0:T(8,128)}), f32[32,8,768]{2,1,0:T(8,128)S(1)}, u32[]{:S(2)}, u32[]{:S(2)}) async-start(f32[32,8,768]{2,1,0:T(8,128)} %bitcast.74), calls=%async_computation | async-start | bytes 1572864 | tf_op jit(solution)/shard_map/all_to_all | solution.py:152
  273.6 15.1 %collective-permute-start.19 = (f32[64,512]{1,0:T(8,128)S(1)}, f32[64,512]{1,0:T(8,128)S(1)}, u32[]{:S(2)}, u32[]{:S(2)}) collective-permute-start(f32[64,512]{1,0:T(8,128)S(1)} %get-tuple-element.27), channel_id=1, source_target_pairs={{0,1},{1,9},{2,17},{3,25},{4,33},{5,41},{6,49},{7,57},{8,65},{9,73... | collective-permute-start | bytes 393224 | tf_op jit(solution)/shard_map/ppermute | solution.py:187
  295.2 24.3 %collective-permute-start.71 = (f32[64,512]{1,0:T(8,128)S(1)}, f32[64,512]{1,0:T(8,128)S(1)}, u32[]{:S(2)}, u32[]{:S(2)}) collective-permute-start(f32[64,512]{1,0:T(8,128)S(1)} %add_add_fusion), channel_id=1, source_target_pairs={{0,0},{1,32},{2,64},{3,96},{4,128},{5,160},{6,192},{7,224},{8,1},{... | collective-permute-start | bytes 393224 | tf_op jit(solution)/shard_map/ppermute | solution.py:131
  306.2 18.6 %collective-permute-start.28 = (f32[64,512]{1,0:T(8,128)S(1)}, f32[64,512]{1,0:T(8,128)S(1)}, u32[]{:S(2)}, u32[]{:S(2)}) collective-permute-start(f32[64,512]{1,0:T(8,128)S(1)} %add_add_fusion), channel_id=1, source_target_pairs={{0,8},{1,3},{2,10},{3,5},{4,12},{5,7},{6,14},{7,1},{8,16},{9,11},{... | collective-permute-start | bytes 393224 | tf_op jit(solution)/shard_map/ppermute | solution.py:100
  312.1 14.0 %collective-permute-start.27 = (f32[64,512]{1,0:T(8,128)S(1)}, f32[64,512]{1,0:T(8,128)S(1)}, u32[]{:S(2)}, u32[]{:S(2)}) collective-permute-start(f32[64,512]{1,0:T(8,128)S(1)} %add_add_fusion), channel_id=1, source_target_pairs={{0,16},{1,5},{2,18},{3,7},{4,20},{5,1},{6,22},{7,3},{8,24},{9,13},... | collective-permute-start | bytes 393224 | tf_op jit(solution)/shard_map/ppermute | solution.py:99
  333.6 55.8 %collective-permute-start.31 = (f32[256,512]{1,0:T(8,128)S(1)}, f32[256,512]{1,0:T(8,128)S(1)}, u32[]{:S(2)}, u32[]{:S(2)}) collective-permute-start(f32[256,512]{1,0:T(8,128)S(1)} %pad_maximum_fusion.2.refs_0_), channel_id=1, source_target_pairs={{0,2},{1,9},{2,4},{3,11},{4,6},{5,13},{6,0},{7,15},{8,10},{9,17},{... | collective-permute-start | bytes 1572872 | tf_op jit(solution)/shard_map/ppermute | solution.py:100
  336.6 14.7 %collective-permute-start.74 = (f32[64,512]{1,0:T(8,128)S(1)}, f32[64,512]{1,0:T(8,128)S(1)}, u32[]{:S(2)}, u32[]{:S(2)}) collective-permute-start(f32[64,512]{1,0:T(8,128)S(1)} %collective-permute-done.71.refs_0_), channel_id=1, source_target_pairs={{0,96},{32,128},{64,160},{96,192},{128,224},{160,0},{192,32},{224,... | collective-permute-start | bytes 393224 | tf_op jit(solution)/shard_map/ppermute | solution.py:124
  339.8 61.5 %collective-permute-start.30 = (f32[256,512]{1,0:T(8,128)S(1)}, f32[256,512]{1,0:T(8,128)S(1)}, u32[]{:S(2)}, u32[]{:S(2)}) collective-permute-start(f32[256,512]{1,0:T(8,128)S(1)} %pad_maximum_fusion.2.refs_0_), channel_id=1, source_target_pairs={{0,4},{1,17},{2,6},{3,19},{4,0},{5,21},{6,2},{7,23},{8,12},{9,25},... | collective-permute-start | bytes 1572872 | tf_op jit(solution)/shard_map/ppermute | solution.py:99
  342.4 107.1 %collective-permute-start.29 = (f32[256,512]{1,0:T(8,128)S(1)}, f32[256,512]{1,0:T(8,128)}, u32[]{:S(2)}, u32[]{:S(2)}) collective-permute-start(f32[256,512]{1,0:T(8,128)S(1)} %pad_maximum_fusion.2.refs_0_), channel_id=1, source_target_pairs={{0,6},{1,25},{2,0},{3,27},{4,2},{5,29},{6,4},{7,31},{8,14},{9,1},{... | collective-permute-start | bytes 1572872 | tf_op jit(solution)/shard_map/ppermute | solution.py:98
  360.5 17.0 %collective-permute-start.72 = (f32[64,512]{1,0:T(8,128)S(1)}, f32[64,512]{1,0:T(8,128)S(1)}, u32[]{:S(2)}, u32[]{:S(2)}) collective-permute-start(f32[64,512]{1,0:T(8,128)S(1)} %collective-permute-done.71.refs_0_), channel_id=1, source_target_pairs={{0,32},{32,64},{64,96},{96,128},{128,160},{160,192},{192,224},{224... | collective-permute-start | bytes 393224 | tf_op jit(solution)/shard_map/ppermute | solution.py:124
  363.3 40.1 %collective-permute-start.66 = (f32[32,768]{1,0:T(8,128)S(1)}, f32[32,768]{1,0:T(8,128)S(1)}, u32[]{:S(2)}, u32[]{:S(2)}) collective-permute-start(f32[32,768]{1,0:T(8,128)S(1)} %pad_maximum_fusion.6.refs_0_), channel_id=1, source_target_pairs={{0,2},{1,9},{2,4},{3,11},{4,6},{5,13},{6,0},{7,15},{8,10},{9,17},{... | collective-permute-start | bytes 294920 | tf_op jit(solution)/shard_map/ppermute | solution.py:100
  377.6 25.9 %collective-permute-start.65 = (f32[32,768]{1,0:T(8,128)S(1)}, f32[32,768]{1,0:T(8,128)S(1)}, u32[]{:S(2)}, u32[]{:S(2)}) collective-permute-start(f32[32,768]{1,0:T(8,128)S(1)} %pad_maximum_fusion.6.refs_0_), channel_id=1, source_target_pairs={{0,4},{1,17},{2,6},{3,19},{4,0},{5,21},{6,2},{7,23},{8,12},{9,25},... | collective-permute-start | bytes 294920 | tf_op jit(solution)/shard_map/ppermute | solution.py:99
  389.4 24.3 %collective-permute-start.64 = (f32[32,768]{1,0:T(8,128)S(1)}, f32[32,768]{1,0:T(8,128)S(1)}, u32[]{:S(2)}, u32[]{:S(2)}) collective-permute-start(f32[32,768]{1,0:T(8,128)S(1)} %pad_maximum_fusion.6.refs_0_), channel_id=1, source_target_pairs={{0,6},{1,25},{2,0},{3,27},{4,2},{5,29},{6,4},{7,31},{8,14},{9,1},{... | collective-permute-start | bytes 294920 | tf_op jit(solution)/shard_map/ppermute | solution.py:98
  401.3 48.4 %collective-permute-start.67 = (f32[32,768]{1,0:T(8,128)S(1)}, f32[32,768]{1,0:T(8,128)S(1)}, u32[]{:S(2)}, u32[]{:S(2)}) collective-permute-start(f32[32,768]{1,0:T(8,128)S(1)} %pad_maximum_fusion.6.refs_0_), channel_id=1, source_target_pairs={{0,1},{1,0},{2,3},{3,2},{4,5},{5,4},{6,7},{7,6},{8,9},{9,8},{10,11... | collective-permute-start | bytes 294920 | tf_op jit(solution)/shard_map/ppermute | solution.py:104
  403.4 46.9 %collective-permute-start.70 = (f32[32,768]{1,0:T(8,128)S(1)}, f32[32,768]{1,0:T(8,128)}, u32[]{:S(2)}, u32[]{:S(2)}) collective-permute-start(f32[32,768]{1,0:T(8,128)S(1)} %collective-permute-done.66.refs_3_), channel_id=1, source_target_pairs={{0,1},{1,0},{2,3},{3,2},{4,5},{5,4},{6,7},{7,6},{8,9},{9,8},{10,11... | collective-permute-start | bytes 294920 | tf_op jit(solution)/shard_map/ppermute | solution.py:104
  403.5 46.9 %collective-permute-start.69 = (f32[32,768]{1,0:T(8,128)S(1)}, f32[32,768]{1,0:T(8,128)}, u32[]{:S(2)}, u32[]{:S(2)}) collective-permute-start(f32[32,768]{1,0:T(8,128)S(1)} %collective-permute-done.65.refs_2_), channel_id=1, source_target_pairs={{0,1},{1,0},{2,3},{3,2},{4,5},{5,4},{6,7},{7,6},{8,9},{9,8},{10,11... | collective-permute-start | bytes 294920 | tf_op jit(solution)/shard_map/ppermute | solution.py:104
  413.7 37.1 %collective-permute-start.68 = (f32[32,768]{1,0:T(8,128)S(1)}, f32[32,768]{1,0:T(8,128)}, u32[]{:S(2)}, u32[]{:S(2)}) collective-permute-start(f32[32,768]{1,0:T(8,128)S(1)} %collective-permute-done.64.refs_1_), channel_id=1, source_target_pairs={{0,1},{1,0},{2,3},{3,2},{4,5},{5,4},{6,7},{7,6},{8,9},{9,8},{10,11... | collective-permute-start | bytes 294920 | tf_op jit(solution)/shard_map/ppermute | solution.py:104
  449.5 98.7 %collective-permute-start.32 = (f32[256,512]{1,0:T(8,128)S(1)}, f32[256,512]{1,0:T(8,128)}, u32[]{:S(2)}, u32[]{:S(2)}) collective-permute-start(f32[256,512]{1,0:T(8,128)S(1)} %pad_maximum_fusion.2.refs_0_), channel_id=1, source_target_pairs={{0,1},{1,0},{2,3},{3,2},{4,5},{5,4},{6,7},{7,6},{8,9},{9,8},{10,11... | collective-permute-start | bytes 1572872 | tf_op jit(solution)/shard_map/ppermute | solution.py:104
  449.6 98.5 %collective-permute-start.35 = (f32[256,512]{1,0:T(8,128)S(1)}, f32[256,512]{1,0:T(8,128)}, u32[]{:S(2)}, u32[]{:S(2)}) collective-permute-start(f32[256,512]{1,0:T(8,128)S(1)} %collective-permute-done.31.refs_3_), channel_id=1, source_target_pairs={{0,1},{1,0},{2,3},{3,2},{4,5},{5,4},{6,7},{7,6},{8,9},{9,8},{10,11... | collective-permute-start | bytes 1572872 | tf_op jit(solution)/shard_map/ppermute | solution.py:104
  450.3 97.9 %collective-permute-start.34 = (f32[256,512]{1,0:T(8,128)S(1)}, f32[256,512]{1,0:T(8,128)}, u32[]{:S(2)}, u32[]{:S(2)}) collective-permute-start(f32[256,512]{1,0:T(8,128)S(1)} %collective-permute-done.30.refs_2_), channel_id=1, source_target_pairs={{0,1},{1,0},{2,3},{3,2},{4,5},{5,4},{6,7},{7,6},{8,9},{9,8},{10,11... | collective-permute-start | bytes 1572872 | tf_op jit(solution)/shard_map/ppermute | solution.py:104
  450.4 97.7 %collective-permute-start.33 = (f32[256,512]{1,0:T(8,128)}, f32[256,512]{1,0:T(8,128)}, u32[]{:S(2)}, u32[]{:S(2)}) collective-permute-start(f32[256,512]{1,0:T(8,128)} %collective-permute-done.29.refs_1_), channel_id=1, source_target_pairs={{0,1},{1,0},{2,3},{3,2},{4,5},{5,4},{6,7},{7,6},{8,9},{9,8},{10,11... | collective-permute-start | bytes 1572872 | tf_op jit(solution)/shard_map/ppermute | solution.py:104
  683.6 116.1 %all-to-all-start.1 = ((f32[32,8,512]{2,1,0:T(8,128)}), f32[32,8,512]{2,1,0:T(8,128)S(1)}, u32[]{:S(2)}, u32[]{:S(2)}) async-start(f32[32,8,512]{2,1,0:T(8,128)} %maximum_bitcast_fusion.1), calls=%async_computation.1 | async-start | bytes 1048576 | tf_op jit(solution)/shard_map/all_to_all | solution.py:152
  689.1 64.8 %collective-permute-start.37 = (f32[64,256]{1,0:T(8,128)S(1)}, f32[64,256]{1,0:T(8,128)S(1)}, u32[]{:S(2)}, u32[]{:S(2)}) collective-permute-start(f32[64,256]{1,0:T(8,128)S(1)} %get-tuple-element.35), channel_id=1, source_target_pairs={{0,1},{1,9},{2,17},{3,25},{4,33},{5,41},{6,49},{7,57},{8,65},{9,73... | collective-permute-start | bytes 196616 | tf_op jit(solution)/shard_map/ppermute | solution.py:202
  702.2 64.8 %collective-permute-start.43 = (f32[64,256]{1,0:T(8,128)S(1)}, f32[64,256]{1,0:T(8,128)S(1)}, u32[]{:S(2)}, u32[]{:S(2)}) collective-permute-start(f32[64,256]{1,0:T(8,128)S(1)} %get-tuple-element.36), channel_id=1, source_target_pairs={{0,7},{1,15},{2,23},{3,31},{4,39},{5,47},{6,55},{7,63},{8,71},{9,7... | collective-permute-start | bytes 196616 | tf_op jit(solution)/shard_map/ppermute | solution.py:202
  715.4 65.0 %collective-permute-start.42 = (f32[64,256]{1,0:T(8,128)S(1)}, f32[64,256]{1,0:T(8,128)S(1)}, u32[]{:S(2)}, u32[]{:S(2)}) collective-permute-start(f32[64,256]{1,0:T(8,128)S(1)} %get-tuple-element.37), channel_id=1, source_target_pairs={{0,6},{1,14},{2,22},{3,30},{4,38},{5,46},{6,54},{7,62},{8,70},{9,7... | collective-permute-start | bytes 196616 | tf_op jit(solution)/shard_map/ppermute | solution.py:202
  728.9 55.4 %collective-permute-start.41 = (f32[64,256]{1,0:T(8,128)S(1)}, f32[64,256]{1,0:T(8,128)S(1)}, u32[]{:S(2)}, u32[]{:S(2)}) collective-permute-start(f32[64,256]{1,0:T(8,128)S(1)} %get-tuple-element.38), channel_id=1, source_target_pairs={{0,5},{1,13},{2,21},{3,29},{4,37},{5,45},{6,53},{7,61},{8,69},{9,7... | collective-permute-start | bytes 196616 | tf_op jit(solution)/shard_map/ppermute | solution.py:202
  742.0 42.3 %collective-permute-start.40 = (f32[64,256]{1,0:T(8,128)S(1)}, f32[64,256]{1,0:T(8,128)S(1)}, u32[]{:S(2)}, u32[]{:S(2)}) collective-permute-start(f32[64,256]{1,0:T(8,128)S(1)} %get-tuple-element.39), channel_id=1, source_target_pairs={{0,4},{1,12},{2,20},{3,28},{4,36},{5,44},{6,52},{7,60},{8,68},{9,7... | collective-permute-start | bytes 196616 | tf_op jit(solution)/shard_map/ppermute | solution.py:202
  753.9 30.4 %collective-permute-start.39 = (f32[64,256]{1,0:T(8,128)S(1)}, f32[64,256]{1,0:T(8,128)S(1)}, u32[]{:S(2)}, u32[]{:S(2)}) collective-permute-start(f32[64,256]{1,0:T(8,128)S(1)} %get-tuple-element.40), channel_id=1, source_target_pairs={{0,3},{1,11},{2,19},{3,27},{4,35},{5,43},{6,51},{7,59},{8,67},{9,7... | collective-permute-start | bytes 196616 | tf_op jit(solution)/shard_map/ppermute | solution.py:202
  767.1 28.7 %collective-permute-start.38 = (f32[64,256]{1,0:T(8,128)S(1)}, f32[64,256]{1,0:T(8,128)S(1)}, u32[]{:S(2)}, u32[]{:S(2)}) collective-permute-start(f32[64,256]{1,0:T(8,128)S(1)} %get-tuple-element.41), channel_id=1, source_target_pairs={{0,2},{1,10},{2,18},{3,26},{4,34},{5,42},{6,50},{7,58},{8,66},{9,7... | collective-permute-start | bytes 196616 | tf_op jit(solution)/shard_map/ppermute | solution.py:202
  780.4 15.4 %collective-permute-start.36 = (f32[64,256]{1,0:T(8,128)S(1)}, f32[64,256]{1,0:T(8,128)S(1)}, u32[]{:S(2)}, u32[]{:S(2)}) collective-permute-start(f32[64,256]{1,0:T(8,128)S(1)} %get-tuple-element.42), channel_id=1, source_target_pairs={{0,0},{1,8},{2,16},{3,24},{4,32},{5,40},{6,48},{7,56},{8,64},{9,72... | collective-permute-start | bytes 196616 | tf_op jit(solution)/shard_map/ppermute | solution.py:202
  795.8 15.0 %collective-permute-start.96 = (f32[64,256]{1,0:T(8,128)S(1)}, f32[64,256]{1,0:T(8,128)S(1)}, u32[]{:S(2)}, u32[]{:S(2)}) collective-permute-start(f32[64,256]{1,0:T(8,128)S(1)} %add_add_fusion.1), channel_id=1, source_target_pairs={{0,0},{1,32},{2,64},{3,96},{4,128},{5,160},{6,192},{7,224},{8,1},{... | collective-permute-start | bytes 196616 | tf_op jit(solution)/shard_map/ppermute | solution.py:131
  798.8 17.5 %collective-permute-start.46 = (f32[64,256]{1,0:T(8,128)S(1)}, f32[64,256]{1,0:T(8,128)S(1)}, u32[]{:S(2)}, u32[]{:S(2)}) collective-permute-start(f32[64,256]{1,0:T(8,128)S(1)} %add_add_fusion.1), channel_id=1, source_target_pairs={{0,8},{1,3},{2,10},{3,5},{4,12},{5,7},{6,14},{7,1},{8,16},{9,11},{... | collective-permute-start | bytes 196616 | tf_op jit(solution)/shard_map/ppermute | solution.py:100
  799.8 16.5 %collective-permute-start.85 = (f32[8,512]{1,0:T(8,128)S(1)}, f32[8,512]{1,0:T(8,128)S(1)}, u32[]{:S(2)}, u32[]{:S(2)}) collective-permute-start(f32[8,512]{1,0:T(8,128)S(1)} %reduce_sum.19), channel_id=1, source_target_pairs={{0,224},{32,0},{64,32},{96,64},{128,96},{160,128},{192,160},{224,1... | collective-permute-start | bytes 49160 | tf_op jit(solution)/shard_map/ppermute | solution.py:139
  838.0 16.2 %collective-permute-start.50 = (f32[256,256]{1,0:T(8,128)S(1)}, f32[256,256]{1,0:T(8,128)S(1)}, u32[]{:S(2)}, u32[]{:S(2)}) collective-permute-start(f32[256,256]{1,0:T(8,128)S(1)} %pad_maximum_fusion.3.refs_0_), channel_id=1, source_target_pairs={{0,1},{1,0},{2,3},{3,2},{4,5},{5,4},{6,7},{7,6},{8,9},{9,8},{10,11... | collective-permute-start | bytes 786440 | tf_op jit(solution)/shard_map/ppermute | solution.py:104
  859.9 24.9 %collective-permute-start.51 = (f32[256,256]{1,0:T(8,128)}, f32[256,256]{1,0:T(8,128)}, u32[]{:S(2)}, u32[]{:S(2)}) collective-permute-start(f32[256,256]{1,0:T(8,128)} %collective-permute-done.47.refs_1_), channel_id=1, source_target_pairs={{0,1},{1,0},{2,3},{3,2},{4,5},{5,4},{6,7},{7,6},{8,9},{9,8},{10,11... | collective-permute-start | bytes 786440 | tf_op jit(solution)/shard_map/ppermute | solution.py:104
  864.1 86.3 %collective-permute-start.92 = (f32[32,512]{1,0:T(8,128)S(1)}, f32[32,512]{1,0:T(8,128)S(1)}, u32[]{:S(2)}, u32[]{:S(2)}) collective-permute-start(f32[32,512]{1,0:T(8,128)S(1)} %pad_maximum_fusion.7.refs_0_), channel_id=1, source_target_pairs={{0,1},{1,0},{2,3},{3,2},{4,5},{5,4},{6,7},{7,6},{8,9},{9,8},{10,11... | collective-permute-start | bytes 196616 | tf_op jit(solution)/shard_map/ppermute | solution.py:104
  864.3 86.1 %collective-permute-start.95 = (f32[32,512]{1,0:T(8,128)}, f32[32,512]{1,0:T(8,128)}, u32[]{:S(2)}, u32[]{:S(2)}) collective-permute-start(f32[32,512]{1,0:T(8,128)} %collective-permute-done.91.refs_3_), channel_id=1, source_target_pairs={{0,1},{1,0},{2,3},{3,2},{4,5},{5,4},{6,7},{7,6},{8,9},{9,8},{10,11... | collective-permute-start | bytes 196616 | tf_op jit(solution)/shard_map/ppermute | solution.py:104
  864.9 85.5 %collective-permute-start.94 = (f32[32,512]{1,0:T(8,128)}, f32[32,512]{1,0:T(8,128)}, u32[]{:S(2)}, u32[]{:S(2)}) collective-permute-start(f32[32,512]{1,0:T(8,128)} %collective-permute-done.90.refs_2_), channel_id=1, source_target_pairs={{0,1},{1,0},{2,3},{3,2},{4,5},{5,4},{6,7},{7,6},{8,9},{9,8},{10,11... | collective-permute-start | bytes 196616 | tf_op jit(solution)/shard_map/ppermute | solution.py:104
  865.1 85.4 %collective-permute-start.93 = (f32[32,512]{1,0:T(8,128)}, f32[32,512]{1,0:T(8,128)}, u32[]{:S(2)}, u32[]{:S(2)}) collective-permute-start(f32[32,512]{1,0:T(8,128)} %collective-permute-done.89.refs_1_), channel_id=1, source_target_pairs={{0,1},{1,0},{2,3},{3,2},{4,5},{5,4},{6,7},{7,6},{8,9},{9,8},{10,11... | collective-permute-start | bytes 196616 | tf_op jit(solution)/shard_map/ppermute | solution.py:104
  (116 other events, 2598.0 us)

commit v2 on v0

v2 whole, which is shorter than its diff:
```python
import jax
import jax.numpy as jnp
from jax import lax
from jax.sharding import PartitionSpec as P

NS_STEPS = 8
ROWS = 8
COLS = 32
BOTH = ("row", "col")


def product(left, right):
    return jnp.dot(left, right, precision=lax.Precision.HIGHEST, preferred_element_type=jnp.float32)


def product3(left, right):
    return jnp.dot(left, right, precision=lax.Precision.HIGH, preferred_element_type=jnp.float32)


def right_solve(factor, values):
    return lax.linalg.triangular_solve(
        factor, values, left_side=False, lower=True, transpose_a=True
    )


def newton_inverse_of_shifted(top):
    size = top.shape[0]
    residual = -top
    approx = jnp.eye(size, dtype=jnp.float32) + residual
    for step in range(1, NS_STEPS):
        residual = product(residual, residual)
        approx = approx + product(approx, residual)
    return approx


def share(block, axis, size):
    parts = lax.all_to_all(jnp.tile(block, (size, 1)), axis, 0, 0, tiled=True)
    return parts.reshape((size,) + block.shape)


def gather_small(block, axis, size):
    return share(block, axis, size).reshape(size * block.shape[0], block.shape[1])


def scatter_sum(block, axis, size):
    parts = lax.all_to_all(block, axis, 0, 0, tiled=True)
    return jnp.sum(parts.reshape(size, block.shape[0] // size, block.shape[1]), axis=0)


def to_columns(block):
    return lax.ppermute(
        block, BOTH, [(at, (at % 8) * COLS + at // 8) for at in range(ROWS * COLS)]
    )


def to_panel(block):
    return lax.ppermute(
        block, BOTH, [((at % 8) * COLS + at // 8, at) for at in range(ROWS * COLS)]
    )


def scatter_from_first_row(block):
    size = block.shape[0] // ROWS
    total = jnp.where(lax.axis_index("row") == 0, block[:size], 0.0)
    for at in range(1, ROWS):
        total = total + lax.ppermute(block[at * size : (at + 1) * size], "row", [(0, at)])
    return total


def shards(a_trail, a_panel, l_panel, a_diag, l_inverse):
    row_dev, col_dev = a_trail.shape
    nb = a_diag.shape[0]
    part = col_dev // ROWS
    row = lax.axis_index("row")
    col = lax.axis_index("col")

    raw_rows = lax.all_gather(jnp.concatenate([a_panel, l_panel], 1), "col", axis=0, tiled=True)

    a11_new = product(product(l_inverse, a_diag), l_inverse.T)
    half_term = 0.5 * product(l_panel, a11_new)
    first_y = product(a_panel, l_inverse.T) - half_term
    panel_out = first_y - half_term
    mates = gather_small(
        to_columns(jnp.concatenate([product(l_panel, l_inverse), panel_out], 1)), "row", ROWS
    )
    updated = a_trail - product3(raw_rows, mates.T)

    local = lax.iota(jnp.int32, col_dev)
    not_top = jnp.logical_or(col > 0, local >= nb)
    head = updated[: 2 * nb]
    panel_t = jnp.where(not_top[None, :], head[:nb], 0.0)

    shard = scatter_from_first_row(jnp.concatenate([panel_t, head[nb:]], 0).T)
    both_rows = lax.all_gather(to_panel(shard), "col", axis=0, tiled=True)
    panel_rows, second_rows = both_rows[:, :nb], both_rows[:, nb:]

    corner = jnp.where(col == 0, head[nb:], 0.0)
    packed = scatter_sum(
        jnp.concatenate([product(panel_t, panel_t.T), corner], 1), "col", COLS
    )
    packed = gather_small(share(packed, "row", ROWS)[0], "col", COLS)
    gram, top_block, corner = packed[:, :nb], packed[:, nb : 2 * nb], packed[:, 2 * nb :]

    partial = product3(updated.T, panel_rows)
    image = scatter_sum(partial, "row", ROWS)
    image_rows = lax.all_gather(to_panel(image), "col", axis=0, tiled=True)
    cols = lax.all_gather(jnp.concatenate([shard, image], 1), "row", axis=0, tiled=True)
    panel_cols, second_cols, image_cols = cols[:, :nb], cols[:, nb : 2 * nb], cols[:, 2 * nb :]

    weights = jnp.concatenate(
        [product(shard[:, :nb].T, image), jnp.where(col == 0, partial[nb : 2 * nb], 0.0)], 1
    )
    weights = scatter_sum(weights, "col", COLS)
    weights = gather_small(jnp.sum(share(weights, "row", ROWS), axis=0), "col", COLS)
    core, image_top = weights[:, :nb], weights[:, nb:]

    factor = jnp.linalg.cholesky(gram)
    solve = right_solve(factor, jnp.eye(nb, dtype=jnp.float32))
    g_inverse = newton_inverse_of_shifted(product(top_block, solve)).T
    image_top = product(image_top, solve)
    middle = product(product(solve.T, core), solve) + image_top + image_top.T + corner
    m_core = product(g_inverse.T, product(middle, g_inverse))
    solve_g = product(solve, g_inverse)

    def reflectors(panel, image, second, owner):
        size = panel.shape[0]
        picker = jnp.logical_and(
            lax.iota(jnp.int32, size)[:, None] - nb == lax.iota(jnp.int32, nb)[None, :], owner
        ).astype(jnp.float32)
        y_part = product3(panel, solve) + picker
        x_part = product3(image, solve_g) + product3(second, g_inverse)
        return y_part, x_part - 0.5 * product3(y_part, m_core)

    y_rows, z_rows = reflectors(panel_rows, image_rows, second_rows, row == 0)
    y_cols, z_cols = reflectors(panel_cols, image_cols, second_cols, col == 0)
    trail_out = updated - product3(
        jnp.concatenate([z_rows, y_rows], 1), jnp.concatenate([y_cols, z_cols], 1).T
    )
    return (trail_out, panel_out)


def solution(mesh):
    return jax.shard_map(
        shards,
        mesh=mesh,
        in_specs=(P("row", "col"), P(("row", "col"), None), P(("row", "col"), None), P(), P()),
        out_specs=(P("row", "col"), P(("row", "col"), None)),
        check_vma=False,
    )
```

time: 851 us -> 401 us (0.47)
  waiting for transfers between devices: 677 us -> 133 us
  starting transfers between devices: 1.59 us -> 72.4 us
  blocking collectives: 0 us -> 42.7 us
  matrix products: 68.9 us -> 56.1 us
    psum x7 -> x0, waiting for transfers between devices: 574 us -> none  [the longest x4 326 us: from_root(): return lax.psum(block, axis)]
    all_gather x2 -> x4, waiting for transfers between devices: 102 us -> 13 us  [the longest x1 13 us: shards(): image_rows = lax.all_gather(to_panel(image), 'col', axis=0, tiled=True)]
    all_to_all x0 -> x6, waiting for transfers between devices: none -> 83.8 us  [the longest x4 57.9 us: share(): parts = lax.all_to_all(jnp.tile(block, (size, 1)), axis, 0, 0, tiled=True)]
    dot_general x31 -> x28, matrix products: 61.7 us -> 16.3 us  [product(): jnp.dot(left, right, precision=lax.Precision.HIGHEST, preferred_element_t...]
    all_to_all x0 -> x6, starting transfers between devices: none -> 45.1 us  [the longest x4 32.8 us: share(): parts = lax.all_to_all(jnp.tile(block, (size, 1)), axis, 0, 0, tiled=True)]
    all_to_all x0 -> x2, blocking collectives: none -> 42.7 us  [the longest x1 28 us: scatter_sum(): parts = lax.all_to_all(block, axis, 0, 0, tiled=True)]
    dot_general x0 -> x11, matrix products: none -> 38.3 us  [product3(): jnp.dot(left, right, precision=lax.Precision.HIGH, preferred_element_type...]
    ppermute x0 -> x10, waiting for transfers between devices: none -> 35.7 us  [the longest x2 22.3 us: to_panel(): lax.ppermute(block, BOTH, [(at % 8 * COLS + at // 8, at) for at in range(...]
  transfers between devices with their start and end apart: 9 -> 20, of which waited for: 9 -> 12; matrix products, arithmetic and copies ran while one was open for 2% -> 24% of each run, Pallas kernels for 0% -> 0%
where the time goes in v2:
time: 401 us; the launch traced here: 394 us
  waiting for transfers between devices  133 us (33%)
  starting transfers between devices  72.4 us (18%)
  other arithmetic  59.5 us (15%)
  matrix products  56.1 us (14%)
  blocking collectives  42.7 us (11%)
  between operations  16.1 us (4%)
  local copies, waits for them, and re-layouts  15 us (4%)
    all_to_all x4, waiting for transfers between devices, share(): parts = lax.all_to_all(jnp.tile(block, (size, 1)), axis, 0, 0, tiled=True)  57.9 us
    dot_general x11, matrix products, product3(): jnp.dot(left, right, precision=lax.Precision.HIGH, preferred_element_type...  38.3 us
    another operation x6, other arithmetic, shards(): factor = jnp.linalg.cholesky(gram)  34 us
    all_to_all x4, starting transfers between devices, share(): parts = lax.all_to_all(jnp.tile(block, (size, 1)), axis, 0, 0, tiled=True)  32.8 us
    all_to_all x1, blocking collectives, scatter_sum(): parts = lax.all_to_all(block, axis, 0, 0, tiled=True)  28 us
    all_to_all x2, waiting for transfers between devices, scatter_sum(): parts = lax.all_to_all(block, axis, 0, 0, tiled=True)  25.9 us
    ppermute x2, waiting for transfers between devices, to_panel(): lax.ppermute(block, BOTH, [(at % 8 * COLS + at // 8, at) for at in range(...  22.3 us
    another operation x3, other arithmetic, right_solve(): lax.linalg.triangular_solve(factor, values, left_side=False, lower=True,...  19.9 us
  transfers between devices with their start and end apart: 20, of which 12 were waited for; matrix products, arithmetic and copies ran while one was open for 24% of the time, Pallas kernels for 0%

profile of v2, /device:TPU:1, one launch (start us, length us, event | category | flops | bytes accessed | tf_op | source)
XLA Modules:
  0.0 394.4 jit_solution(14805733286405899376)
XLA Ops:
  7.2 1.6 pad_maximum_fusion.2
  12.4 4.9 %collective-permute-start = (f32[64,512]{1,0:T(8,128)S(1)}, f32[64,512]{1,0:T(8,128)S(1)}, u32[]{:S(2)}, u32[]{:S(2)}) collective-permute-start(f32[64,512]{1,0:T(8,128)S(1)} %pad_maximum_fusion.3), channel_id=1, source_target_pairs={{0,0},{1,32},{2,64},{3,96},{4,128},{5,160},{6,192},{7,224},{8,1},{... | collective-permute-start | bytes 393224 | tf_op jit(solution)/shard_map/ppermute | solution.py:51
  17.4 2.2 collective-permute-done
  20.7 19.3 %all-to-all-start = ((f32[8,64,512]{2,1,0:T(8,128)}), f32[8,64,512]{2,1,0:T(8,128)S(1)}, u32[]{:S(2)}, u32[]{:S(2)}) async-start(f32[8,64,512]{2,1,0:T(8,128)} %tile.12), calls=%async_computation | async-start | bytes 2097152 | tf_op jit(solution)/shard_map/all_to_all | solution.py:37
  40.0 29.2 %all-to-all-done = f32[8,64,512]{2,1,0:T(8,128)S(1)} async-done(((f32[8,64,512]{2,1,0:T(8,128)}), f32[8,64,512]{2,1,0:T(8,128)S(1)}, u32[]{:S(2)}, u32[]{:S(2)}) %all-to-all-start) | async-done | bytes 1048608 | tf_op jit(solution)/shard_map/all_to_all | solution.py:37
  69.2 8.1 %convolution_subtract_fusion = f32[2048,512]{1,0:T(8,128)S(1)} fusion(f32[2048,512]{1,0:T(8,128)} %param.5, f32[2048,512]{1,0:T(8,128)} %all-gather.5.cloned.1.call-done, f32[512,512]{1,0:T(8,128)S(1)} %bitcast.109), kind=kOutput, calls=%fused_computation.7 | convolution fusion | flops 3222274048 | bytes 13631488 | tf_op jit(solution)/shard_map/dot_general | solution.py:17
  77.7 1.7 copy-done.1
  80.4 2.1 collective-permute-start.1
  82.4 1.7 collective-permute-start.2
  84.1 2.4 collective-permute-start.3
  86.5 3.6 collective-permute-start.4
  90.0 2.0 collective-permute-start.5
  92.0 2.0 collective-permute-start.6
  94.8 2.0 collective-permute-start.7
  96.7 2.1 collective-permute-done.3
  98.8 5.5 %collective-permute-done.4 = f32[64,512]{0,1:T(8,128)} collective-permute-done((f32[64,512]{0,1:T(8,128)S(1)}, f32[64,512]{0,1:T(8,128)}, u32[]{:S(2)}, u32[]{:S(2)}) %collective-permute-start.4) | collective-permute-done | bytes 131104 | tf_op jit(solution)/shard_map/ppermute | solution.py:66
  104.4 3.6 collective-permute-done.7
  108.0 1.5 fusion.38
  109.5 3.7 collective-permute-start.8
  113.3 22.3 %collective-permute-done.8 = f32[64,512]{0,1:T(8,128)S(1)} collective-permute-done((f32[64,512]{0,1:T(8,128)S(1)}, f32[64,512]{0,1:T(8,128)S(1)}, u32[]{:S(2)}, u32[]{:S(2)}) %collective-permute-start.8) | collective-permute-done | bytes 131104 | tf_op jit(solution)/shard_map/ppermute | solution.py:57
  137.0 28.0 %all_to_all.66 = f32[32,8,768]{2,1,0:T(8,128)S(1)} all-to-all(f32[32,8,768]{2,1,0:T(8,128)S(1)} %maximum_bitcast_fusion.1), channel_id=1, replica_groups=mesh['row'=8,'col'=32] {'col'}, dimensions={0} | all-to-all | bytes 1572864 | tf_op jit(solution)/shard_map/all_to_all | solution.py:46
  165.1 14.7 %all_to_all.67 = f32[8,8,768]{2,1,0:T(8,128)S(1)} all-to-all(f32[8,8,768]{2,1,0:T(8,128)S(1)} %tile.13), channel_id=1, replica_groups=mesh['row'=8,'col'=32] {'row'}, dimensions={0} | all-to-all | bytes 393216 | tf_op jit(solution)/shard_map/all_to_all | solution.py:37
  180.7 4.3 %all-to-all-start.4 = ((f32[32,8,768]{2,1,0:T(8,128)}), f32[32,8,768]{2,1,0:T(8,128)S(1)}, u32[]{:S(2)}, u32[]{:S(2)}) async-start(f32[32,8,768]{2,1,0:T(8,128)} %tile.15), calls=%async_computation.4 | async-start | bytes 1572864 | tf_op jit(solution)/shard_map/all_to_all | solution.py:37
  185.1 14.3 %all-to-all-done.4 = f32[32,8,768]{2,1,0:T(8,128)S(1)} async-done(((f32[32,8,768]{2,1,0:T(8,128)}), f32[32,8,768]{2,1,0:T(8,128)S(1)}, u32[]{:S(2)}, u32[]{:S(2)}) %all-to-all-start.4) | async-done | bytes 786464 | tf_op jit(solution)/shard_map/all_to_all | solution.py:37
  199.6 11.7 %cholesky.50 = f32[128,128]{1,0:T(8,128)S(1)} custom-call(f32[128,128]{1,0:T(8,128)S(1)} %cholesky.118), custom_call_target="Cholesky" | custom-call | tf_op jit(solution)/shard_map/jit(cholesky)/cholesky | solution.py:117
  211.3 9.8 %custom-call.14 = f32[1,128,128]{1,2,0:T(8,128)S(1)} custom-call(f32[1,128,128]{2,1,0:T(8,128)S(1)} %get-tuple-element.33), custom_call_target="InvertDiagBlocksLowerTriangular" | custom-call | tf_op jit(solution)/shard_map/jit(cholesky)/cholesky | solution.py:117
  221.6 11.7 %cholesky.105 = f32[128,128]{1,0:T(8,128)S(1)} custom-call(f32[128,128]{1,0:T(8,128)S(1)} %convolution_subtract_fusion.2), custom_call_target="Cholesky" | custom-call | tf_op jit(solution)/shard_map/jit(cholesky)/cholesky | solution.py:117
  235.4 3.8 while.1
  239.2 19.9 %custom-call.15 = f32[2,128,128]{1,2,0:T(8,128)S(1)} custom-call(f32[2,128,128]{2,1,0:T(8,128)S(1)} %get-tuple-element.9), custom_call_target="InvertDiagBlocksLowerTriangular" | custom-call | tf_op jit(solution)/shard_map/triangular_solve | solution.py:21
  259.7 7.1 %fusion.12 = f32[512,256]{1,0:T(8,128)} fusion(f32[2048,512]{1,0:T(8,128)} %copy-done.1, f32[2048,512]{1,0:T(8,128)} %all-gather.7.cloned.1.call-done), kind=kOutput, calls=%fused_computation.17 | convolution fusion | flops 1610612736 | bytes 6815744 | tf_op jit(solution)/shard_map/dot_general | solution.py:17
  266.9 5.1 %all-to-all-start.1 = ((f32[8,64,256]{2,1,0:T(8,128)}), f32[8,64,256]{2,1,0:T(8,128)S(1)}, u32[]{:S(2)}, u32[]{:S(2)}) async-start(f32[8,64,256]{2,1,0:T(8,128)} %bitcast.3), calls=%async_computation.1 | async-start | bytes 1048576 | tf_op jit(solution)/shard_map/all_to_all | solution.py:46
  273.6 16.4 %all-to-all-done.1 = f32[8,64,256]{2,1,0:T(8,128)S(1)} async-done(((f32[8,64,256]{2,1,0:T(8,128)}), f32[8,64,256]{2,1,0:T(8,128)S(1)}, u32[]{:S(2)}, u32[]{:S(2)}) %all-to-all-start.1) | async-done | bytes 524320 | tf_op jit(solution)/shard_map/all_to_all | solution.py:46
  295.4 2.6 collective-permute-start.9
  299.2 7.2 %all-to-all-start.5 = ((f32[32,8,512]{2,1,0:T(8,128)}), f32[32,8,512]{2,1,0:T(8,128)S(1)}, u32[]{:S(2)}, u32[]{:S(2)}) async-start(f32[32,8,512]{2,1,0:T(8,128)} %maximum_bitcast_fusion.2), calls=%async_computation.5 | async-start | bytes 1048576 | tf_op jit(solution)/shard_map/all_to_all | solution.py:46
  308.6 9.5 %all-to-all-done.5 = f32[32,8,512]{2,1,0:T(8,128)S(1)} async-done(((f32[32,8,512]{2,1,0:T(8,128)}), f32[32,8,512]{2,1,0:T(8,128)S(1)}, u32[]{:S(2)}, u32[]{:S(2)}) %all-to-all-start.5) | async-done | bytes 524320 | tf_op jit(solution)/shard_map/all_to_all | solution.py:46
  318.8 5.1 %all-to-all-start.6 = ((f32[8,8,512]{2,1,0:T(8,128)}), f32[8,8,512]{2,1,0:T(8,128)S(1)}, u32[]{:S(2)}, u32[]{:S(2)}) async-start(f32[8,8,512]{2,1,0:T(8,128)} %tile.16), calls=%async_computation.6 | async-start | bytes 262144 | tf_op jit(solution)/shard_map/all_to_all | solution.py:37
  325.2 7.9 %all-to-all-done.6 = f32[8,8,512]{2,1,0:T(8,128)S(1)} async-done(((f32[8,8,512]{2,1,0:T(8,128)}), f32[8,8,512]{2,1,0:T(8,128)S(1)}, u32[]{:S(2)}, u32[]{:S(2)}) %all-to-all-start.6) | async-done | bytes 131104 | tf_op jit(solution)/shard_map/all_to_all | solution.py:37
  333.9 4.2 %all-to-all-start.7 = ((f32[32,8,512]{2,1,0:T(8,128)}), f32[32,8,512]{2,1,0:T(8,128)S(1)}, u32[]{:S(2)}, u32[]{:S(2)}) async-start(f32[32,8,512]{2,1,0:T(8,128)} %tile.17), calls=%async_computation.7 | async-start | bytes 1048576 | tf_op jit(solution)/shard_map/all_to_all | solution.py:37
  338.1 3.0 convolution_add_fusion
  341.1 2.4 fusion.8
  343.5 6.6 %all-to-all-done.7 = f32[32,8,512]{2,1,0:T(8,128)S(1)} async-done(((f32[32,8,512]{2,1,0:T(8,128)}), f32[32,8,512]{2,1,0:T(8,128)S(1)}, u32[]{:S(2)}, u32[]{:S(2)}) %all-to-all-start.7) | async-done | bytes 524320 | tf_op jit(solution)/shard_map/all_to_all | solution.py:37
  356.7 2.4 convolution_multiply_fusion
  359.1 1.5 convolution_add_fusion.3
  360.6 1.5 fusion.23
  362.2 1.5 convolution_add_fusion.2
  365.0 13.0 %all-gather.9.cloned.1.call-done = f32[2048,256]{1,0:T(8,128)} async-done(((f32[64,256]{1,0:T(8,128)}), f32[2048,256]{1,0:T(8,128)}) %all-gather.9.cloned.1.call-update) | async-done | bytes 2097168 | tf_op jit(solution)/shard_map/all_gather | solution.py:106
  378.0 4.2 %fusion.7 = f32[2048,256]{0,1:T(8,128)S(1)} fusion(f32[2048,256]{0,1:T(8,128)} %convolution_multiply_fusion, f32[2048,256]{0,1:T(8,128)} %fusion.8, f32[2048,256]{1,0:T(8,128)} %all-gather.9.cloned.1.call-done, f32[256,256]{1,0:T(8,128)S(1)} %copy-done.5), kind=kOutput, calls=%fused_computation.11 | convolution fusion | flops 806354944 | bytes 8650752 | tf_op jit(solution)/shard_map/dot_general | solution.py:17
  382.2 5.2 %fusion.4 = f32[2048,512]{1,0:T(8,128)} fusion(f32[2048,512]{1,0:T(8,128)S(1)} %copy-done.2, f32[2048,256]{0,1:T(8,128)S(1)} %convolution_add_fusion, f32[2048,256]{0,1:T(8,128)S(1)} %fusion.7, f32[512,256]{0,1:T(8,128)S(1)} %copy-done.9, f32[512,256]{0,1:T(8,128)S(1)} %convolution_add_fusion.3), kind=kOutput, calls=%fused_computation.6 | convolution fusion | flops 3223584768 | bytes 13631488 | tf_op jit(solution)/shard_map/dot_general | solution.py:17
  (126 shorter events, 36.1 us)
Async XLA Ops:
  7.2 1.7 copy-start
  7.2 4.6 %copy-start.10 = (f32[64,256]{1,0:T(8,128)S(1)}, f32[64,256]{1,0:T(8,128)}, u32[]{:S(2)}) copy-start(f32[64,256]{1,0:T(8,128)} %param.7) | copy-start | bytes 196612
  7.2 4.8 %copy-start.13 = (f32[64,256]{1,0:T(8,128)S(1)}, f32[64,256]{1,0:T(8,128)}, u32[]{:S(2)}) copy-start(f32[64,256]{1,0:T(8,128)} %param.6) | copy-start | bytes 196612
  7.2 62.0 %all-gather.5.cloned.1.call-start = ((), (), s32[]{:S(2)}) async-start(), calls=%async_computation.8 | async-start | bytes 4325376 | tf_op jit(solution)/shard_map/all_gather | solution.py:77
  12.4 64.9 %copy-start.14 = (f32[64,256]{1,0:T(8,128)}, f32[64,256]{1,0:T(8,128)S(1)}, u32[]{:S(2)}) copy-start(f32[64,256]{1,0:T(8,128)S(1)} %fusion.18) | copy-start | bytes 196612
  12.4 7.2 %collective-permute-start = (f32[64,512]{1,0:T(8,128)S(1)}, f32[64,512]{1,0:T(8,128)S(1)}, u32[]{:S(2)}, u32[]{:S(2)}) collective-permute-start(f32[64,512]{1,0:T(8,128)S(1)} %pad_maximum_fusion.3), channel_id=1, source_target_pairs={{0,0},{1,32},{2,64},{3,96},{4,128},{5,160},{6,192},{7,224},{8,1},{... | collective-permute-start | bytes 393224 | tf_op jit(solution)/shard_map/ppermute | solution.py:51
  20.7 48.5 %all-to-all-start = ((f32[8,64,512]{2,1,0:T(8,128)}), f32[8,64,512]{2,1,0:T(8,128)S(1)}, u32[]{:S(2)}, u32[]{:S(2)}) async-start(f32[8,64,512]{2,1,0:T(8,128)} %tile.12), calls=%async_computation | async-start | bytes 2097152 | tf_op jit(solution)/shard_map/all_to_all | solution.py:37
  39.9 219.8 %all-gather.7.cloned.1.call-start = ((), (), s32[]{:S(2)}) async-start(), calls=%async_computation.9 | async-start | bytes 4325376 | tf_op jit(solution)/shard_map/all_gather | solution.py:94
  77.4 2.0 copy-start.1
  80.4 11.7 %collective-permute-start.1 = (f32[64,512]{0,1:T(8,128)S(1)}, f32[64,512]{0,1:T(8,128)S(1)}, u32[]{:S(2)}, u32[]{:S(2)}) collective-permute-start(f32[64,512]{0,1:T(8,128)S(1)} %get-tuple-element.23), channel_id=1, source_target_pairs={{0,32},{1,33},{2,34},{3,35},{4,36},{5,37},{6,38},{7,39},{8,40},{9,... | collective-permute-start | bytes 393224 | tf_op jit(solution)/shard_map/ppermute | solution.py:66
  82.4 11.6 %collective-permute-start.2 = (f32[64,512]{0,1:T(8,128)S(1)}, f32[64,512]{0,1:T(8,128)S(1)}, u32[]{:S(2)}, u32[]{:S(2)}) collective-permute-start(f32[64,512]{0,1:T(8,128)S(1)} %get-tuple-element.29), channel_id=1, source_target_pairs={{0,64},{1,65},{2,66},{3,67},{4,68},{5,69},{6,70},{7,71},{8,72},{9,... | collective-permute-start | bytes 393224 | tf_op jit(solution)/shard_map/ppermute | solution.py:66
  84.1 14.7 %collective-permute-start.3 = (f32[64,512]{0,1:T(8,128)}, f32[64,512]{0,1:T(8,128)}, u32[]{:S(2)}, u32[]{:S(2)}) collective-permute-start(f32[64,512]{0,1:T(8,128)} %get-tuple-element.28), channel_id=1, source_target_pairs={{0,96},{1,97},{2,98},{3,99},{4,100},{5,101},{6,102},{7,103},{8,104... | collective-permute-start | bytes 393224 | tf_op jit(solution)/shard_map/ppermute | solution.py:66
  86.5 17.9 %collective-permute-start.4 = (f32[64,512]{0,1:T(8,128)S(1)}, f32[64,512]{0,1:T(8,128)}, u32[]{:S(2)}, u32[]{:S(2)}) collective-permute-start(f32[64,512]{0,1:T(8,128)S(1)} %get-tuple-element.27), channel_id=1, source_target_pairs={{0,128},{1,129},{2,130},{3,131},{4,132},{5,133},{6,134},{7,135},{8... | collective-permute-start | bytes 393224 | tf_op jit(solution)/shard_map/ppermute | solution.py:66
  90.0 14.3 %collective-permute-start.5 = (f32[64,512]{0,1:T(8,128)S(1)}, f32[64,512]{0,1:T(8,128)}, u32[]{:S(2)}, u32[]{:S(2)}) collective-permute-start(f32[64,512]{0,1:T(8,128)S(1)} %get-tuple-element.26), channel_id=1, source_target_pairs={{0,160},{1,161},{2,162},{3,163},{4,164},{5,165},{6,166},{7,167},{8... | collective-permute-start | bytes 393224 | tf_op jit(solution)/shard_map/ppermute | solution.py:66
  92.0 2.0 copy-start.11
  92.0 12.3 %collective-permute-start.6 = (f32[64,512]{0,1:T(8,128)S(1)}, f32[64,512]{0,1:T(8,128)}, u32[]{:S(2)}, u32[]{:S(2)}) collective-permute-start(f32[64,512]{0,1:T(8,128)S(1)} %get-tuple-element.25), channel_id=1, source_target_pairs={{0,192},{1,193},{2,194},{3,195},{4,196},{5,197},{6,198},{7,199},{8... | collective-permute-start | bytes 393224 | tf_op jit(solution)/shard_map/ppermute | solution.py:66
  94.0 0.7 copy-start.12
  94.8 13.2 %collective-permute-start.7 = (f32[64,512]{0,1:T(8,128)S(1)}, f32[64,512]{0,1:T(8,128)}, u32[]{:S(2)}, u32[]{:S(2)}) collective-permute-start(f32[64,512]{0,1:T(8,128)S(1)} %get-tuple-element.24), channel_id=1, source_target_pairs={{0,224},{1,225},{2,226},{3,227},{4,228},{5,229},{6,230},{7,231},{8... | collective-permute-start | bytes 393224 | tf_op jit(solution)/shard_map/ppermute | solution.py:66
  109.5 26.0 %collective-permute-start.8 = (f32[64,512]{0,1:T(8,128)S(1)}, f32[64,512]{0,1:T(8,128)S(1)}, u32[]{:S(2)}, u32[]{:S(2)}) collective-permute-start(f32[64,512]{0,1:T(8,128)S(1)} %fusion.38), channel_id=1, source_target_pairs={{0,0},{32,1},{64,2},{96,3},{128,4},{160,5},{192,6},{224,7},{1,8},{... | collective-permute-start | bytes 393224 | tf_op jit(solution)/shard_map/ppermute | solution.py:57
  180.7 18.6 %all-to-all-start.4 = ((f32[32,8,768]{2,1,0:T(8,128)}), f32[32,8,768]{2,1,0:T(8,128)S(1)}, u32[]{:S(2)}, u32[]{:S(2)}) async-start(f32[32,8,768]{2,1,0:T(8,128)} %tile.15), calls=%async_computation.4 | async-start | bytes 1572864 | tf_op jit(solution)/shard_map/all_to_all | solution.py:37
  199.3 73.0 %copy-start.4 = (f32[32,8,768]{2,1,0:T(8,128)}, f32[32,8,768]{2,1,0:T(8,128)S(1)}, u32[]{:S(2)}) copy-start(f32[32,8,768]{2,1,0:T(8,128)S(1)} %all-to-all-done.4) | copy-start | bytes 2359300
  266.9 23.1 %all-to-all-start.1 = ((f32[8,64,256]{2,1,0:T(8,128)}), f32[8,64,256]{2,1,0:T(8,128)S(1)}, u32[]{:S(2)}, u32[]{:S(2)}) async-start(f32[8,64,256]{2,1,0:T(8,128)} %bitcast.3), calls=%async_computation.1 | async-start | bytes 1048576 | tf_op jit(solution)/shard_map/all_to_all | solution.py:46
  272.0 87.1 %all-gather.11.cloned.1.call-start = ((), (), s32[]{:S(2)}) async-start(), calls=%async_computation.11 | async-start | bytes 1769472 | tf_op jit(solution)/shard_map/all_gather | solution.py:107
  295.4 11.3 %collective-permute-start.9 = (f32[64,256]{1,0:T(8,128)S(1)}, f32[64,256]{1,0:T(8,128)S(1)}, u32[]{:S(2)}, u32[]{:S(2)}) collective-permute-start(f32[64,256]{1,0:T(8,128)S(1)} %reduce_sum.36), channel_id=1, source_target_pairs={{0,0},{32,1},{64,2},{96,3},{128,4},{160,5},{192,6},{224,7},{1,8},{... | collective-permute-start | bytes 196616 | tf_op jit(solution)/shard_map/ppermute | solution.py:57
  299.2 18.8 %all-to-all-start.5 = ((f32[32,8,512]{2,1,0:T(8,128)}), f32[32,8,512]{2,1,0:T(8,128)S(1)}, u32[]{:S(2)}, u32[]{:S(2)}) async-start(f32[32,8,512]{2,1,0:T(8,128)} %maximum_bitcast_fusion.2), calls=%async_computation.5 | async-start | bytes 1048576 | tf_op jit(solution)/shard_map/all_to_all | solution.py:46
  306.4 71.5 %all-gather.9.cloned.1.call-start = ((), (), s32[]{:S(2)}) async-start(), calls=%async_computation.10 | async-start | bytes 2162688 | tf_op jit(solution)/shard_map/all_gather | solution.py:106
  306.7 0.6 copy-start.15
  318.8 14.3 %all-to-all-start.6 = ((f32[8,8,512]{2,1,0:T(8,128)}), f32[8,8,512]{2,1,0:T(8,128)S(1)}, u32[]{:S(2)}, u32[]{:S(2)}) async-start(f32[8,8,512]{2,1,0:T(8,128)} %tile.16), calls=%async_computation.6 | async-start | bytes 262144 | tf_op jit(solution)/shard_map/all_to_all | solution.py:37
  333.9 16.2 %all-to-all-start.7 = ((f32[32,8,512]{2,1,0:T(8,128)}), f32[32,8,512]{2,1,0:T(8,128)S(1)}, u32[]{:S(2)}, u32[]{:S(2)}) async-start(f32[32,8,512]{2,1,0:T(8,128)} %tile.17), calls=%async_computation.7 | async-start | bytes 1048576 | tf_op jit(solution)/shard_map/all_to_all | solution.py:37
  338.1 3.0 copy-start.3
  350.1 0.8 copy-start.8
  356.0 0.7 copy-start.6
  359.1 4.6 %copy-start.7 = (f32[256,256]{1,0:T(8,128)S(1)}, f32[256,256]{1,0:T(8,128)}, u32[]{:S(2)}) copy-start(f32[256,256]{1,0:T(8,128)} %copy-done.6) | copy-start | bytes 786436
  362.2 15.8 %copy-start.5 = (f32[256,256]{1,0:T(8,128)S(1)}, f32[256,256]{1,0:T(8,128)}, u32[]{:S(2)}) copy-start(f32[256,256]{1,0:T(8,128)} %fusion.54) | copy-start | bytes 786436
  378.0 4.2 %copy-start.2 = (f32[2048,512]{1,0:T(8,128)S(1)}, f32[2048,512]{1,0:T(8,128)}, u32[]{:S(2)}) copy-start(f32[2048,512]{1,0:T(8,128)} %copy-done.1) | copy-start | bytes 12582916
  378.0 4.2 %copy-start.9 = (f32[512,256]{0,1:T(8,128)S(1)}, f32[512,256]{0,1:T(8,128)}, u32[]{:S(2)}) copy-start(f32[512,256]{0,1:T(8,128)} %fusion.14) | copy-start | bytes 1572868
Sparse Core Ops, SparseCore 0:
  10.6 57.4 all-gather.4
  136.5 56.7 all-gather.6
  291.1 33.6 all-gather.10
  327.2 50.6 all-gather.8
